TPU v7x, 32 devices: a whole 2x2x4 slice. The times are simulated.
32 devices in a mesh: dir: 2 (over x), shard: 16 (over z, y, core).
Axes of the slice: x: 2, y: 2, z: 4, core: 2. Of those that a mesh axis runs over, the one named last changes fastest.
Arguments:
- propagators: bfloat16 [2, 512, 64, 1024], P('dir', 'shard'), may hold values from 0.5 to 1.5
- field: float32 [64, 1024], replicated, may hold values from -0.5 to 0.5
- orient: float32 [3, 512], replicated, may hold values from -1 to 1, as said below
- quad_weights: float32 [512], replicated, may hold values from 0.01 to 0.1
- analysis: bfloat16 [441, 512], replicated, may hold values from -0.25 to 0.25
- synthesis: bfloat16 [512, 441], replicated, may hold values from -0.4375 to 0.4375
- decay: float32 [441], replicated, may hold values from 0.5 to 1
Outputs:
- density: float32 [64, 1024], P('shard', 'dir')
- qtensor: float32 [5, 64, 1024], P(None, 'shard', 'dir')
Inputs may be any that keep to these rules, and one draw needn't show every extreme that they name: Each column of orient is a unit vector.
All inputs are finite; a program needn't handle non-finite values.
Results may differ from a plain program's by a relative error of at most 0.028.
Values may be sent and summed in bfloat16 or wider, within the bound.
A program may use at most 192 MiB of HBM per device.

v0:
```python
import math

import jax
import jax.numpy as jnp
from jax import lax
from jax.sharding import PartitionSpec as P

NX = 64
NY = 64
NZ = 16
STEPS = 2


transport_length = 1.5
one_third = 1.0 / 3.0
patterns = {1: "kx,mxyz->mkyz", 2: "ky,mxyz->mxkz", 3: "kz,mxyz->mxyk"}


def dft_tables(length):
    counter = jnp.arange(length, dtype=jnp.int32)
    wrapped = counter[:, None] * counter[None, :] % length
    angles = wrapped.astype(jnp.float32) * (2.0 * math.pi / length)
    return (jnp.cos(angles).astype(jnp.bfloat16), jnp.sin(angles).astype(jnp.bfloat16))


def wave_numbers(length):
    counter = jnp.arange(length, dtype=jnp.int32)
    signed = jnp.where(counter <= (length - 1) // 2, counter, counter - length)
    return signed.astype(jnp.float32) * (2.0 * math.pi / length)


def phases(heading, direction, lengths):
    wave_x = wave_numbers(lengths[0])[None, :, None, None]
    wave_y = wave_numbers(lengths[1])[None, None, :, None]
    wave_z = wave_numbers(lengths[2])[None, None, None, :]
    phase_angle = (
        heading[0][:, None, None, None] * wave_x
        + heading[1][:, None, None, None] * wave_y
        + heading[2][:, None, None, None] * wave_z
    ) * (direction * transport_length)
    return (jnp.cos(phase_angle), jnp.sin(phase_angle))


def along_axis(table, values, position):
    return jnp.einsum(patterns[position], table, values, preferred_element_type=jnp.float32)


def complex_pass(tables, real_part, imag_part, position, turning):
    cosine_table, sine_table = tables
    new_real = along_axis(cosine_table, real_part, position) - turning * along_axis(
        sine_table, imag_part, position
    )
    new_imag = along_axis(cosine_table, imag_part, position) + turning * along_axis(
        sine_table, real_part, position
    )
    return (new_real.astype(jnp.bfloat16), new_imag.astype(jnp.bfloat16))


def transport(flat_values, dft_sets, cos_phase, sin_phase, damping):
    values = flat_values.reshape(flat_values.shape[0], NX, NY, NZ)
    cos_x, sin_x = dft_sets[0]
    real_part = along_axis(cos_x, values, 1).astype(jnp.bfloat16)
    imag_part = (-along_axis(sin_x, values, 1)).astype(jnp.bfloat16)
    real_part, imag_part = complex_pass(dft_sets[1], real_part, imag_part, 2, -1.0)
    real_part, imag_part = complex_pass(dft_sets[2], real_part, imag_part, 3, -1.0)
    real_wide = real_part.astype(jnp.float32)
    imag_wide = imag_part.astype(jnp.float32)
    real_part = (real_wide * cos_phase + imag_wide * sin_phase).astype(jnp.bfloat16)
    imag_part = (imag_wide * cos_phase - real_wide * sin_phase).astype(jnp.bfloat16)
    real_part, imag_part = complex_pass(dft_sets[2], real_part, imag_part, 3, 1.0)
    real_part, imag_part = complex_pass(dft_sets[1], real_part, imag_part, 2, 1.0)
    summed = along_axis(cos_x, real_part, 1) - along_axis(sin_x, imag_part, 1)
    return (summed * damping[None]).astype(jnp.bfloat16).reshape(flat_values.shape)


def diffuse(points, analysis, synthesis, decay):
    layout = points.shape
    columns = points.reshape(layout[0], -1)
    harmonic_part = jnp.dot(analysis, columns, preferred_element_type=jnp.float32)
    harmonic_part = (harmonic_part * decay[:, None]).astype(jnp.bfloat16)
    return (
        jnp.dot(synthesis, harmonic_part, preferred_element_type=jnp.float32)
        .astype(jnp.bfloat16)
        .reshape(layout)
    )


def moment_table(orient, quad_weights):
    head_x, head_y, head_z = (orient[0], orient[1], orient[2])
    unity = jnp.ones_like(head_x)
    moment_rows = [
        unity,
        head_x * head_x - one_third,
        head_y * head_y - one_third,
        head_x * head_y,
        head_x * head_z,
        head_y * head_z,
    ]
    return jnp.stack(moment_rows) * quad_weights[None, :]


def on_device(propagators, field, orient, quad_weights, analysis, synthesis, decay):
    state = propagators[0]
    local_count = state.shape[0]
    offset = lax.axis_index("shard") * local_count
    heading = lax.dynamic_slice_in_dim(orient, offset, local_count, 1)
    direction = 1.0 - 2.0 * lax.axis_index("dir").astype(jnp.float32)
    cos_phase, sin_phase = phases(heading, direction, (NX, NY, NZ))
    dft_sets = [dft_tables(NX), dft_tables(NY), dft_tables(NZ)]
    damping = jnp.exp(-field.reshape(NX, NY, NZ)) / float(NX * NY * NZ)

    def diffuse_only(points):
        return diffuse(points, analysis, synthesis, decay)

    def diffuse_back(points):
        return lax.all_to_all(
            diffuse_only(points), "shard", split_axis=0, concat_axis=1, tiled=True
        )

    paired = None
    for contour in range(STEPS):
        moved = transport(state, dft_sets, cos_phase, sin_phase, damping)
        is_last = contour == STEPS - 1
        handler = diffuse_only if is_last else diffuse_back
        result = handler(lax.all_to_all(moved, "shard", split_axis=1, concat_axis=0, tiled=True))
        if is_last:
            paired = lax.all_to_all(result[None], "dir", split_axis=3, concat_axis=0, tiled=True)
        else:
            state = result
    orientations = paired.shape[1]
    point_shape = paired.shape[2:]
    forward_part = paired[0].reshape(orientations, -1).astype(jnp.float32)
    backward_part = paired[1].reshape(orientations, -1).astype(jnp.float32)
    product = forward_part * backward_part
    result = jnp.dot(moment_table(orient, quad_weights), product, precision=lax.Precision.HIGHEST)
    return (result[0].reshape(point_shape), result[1:].reshape((5,) + point_shape))


def solution(mesh):
    in_specs = (P("dir", "shard", None, None), P(), P(), P(), P(), P(), P())
    out_specs = (P("shard", "dir"), P(None, "shard", "dir"))
    return jax.shard_map(
        on_device, mesh=mesh, in_specs=in_specs, out_specs=out_specs, check_vma=False
    )
```

profile of v0, /device:TPU:19, one launch (start us, length us, event | category | flops | bytes accessed | tf_op | source)
XLA Modules:
  0.0 1436.4 jit_solution(3203220807061475494)
XLA Ops:
  56.4 13.6 fusion.57
  70.0 14.2 fusion.49
  84.2 13.8 fusion.54
  98.0 14.2 fusion.51
  112.3 18.4 %add_convert_fusion.6 = bf16[32,64,64,16]{2,3,1,0:T(8,128)(2,1)} fusion(f32[32,64,64,16]{2,3,1,0:T(8,128)} %fusion.49, bf16[32,64,64,16]{2,1,3,0:T(8,128)(2,1)} %fusion.54), kind=kOutput, calls=%fused_computation.33 | convolution fusion | flops 73404160 | bytes 16777216 | tf_op jit(solution)/shard_map/kz,mxyz->mxyk/dot_general | solution.py:45
  130.7 18.7 %subtract_convert_fusion.6 = bf16[32,64,64,16]{2,3,1,0:T(8,128)(2,1)} fusion(f32[32,64,64,16]{2,3,1,0:T(8,128)} %fusion.51, bf16[32,64,64,16]{2,1,3,0:T(8,128)(2,1)} %fusion.57), kind=kOutput, calls=%fused_computation.37 | convolution fusion | flops 73404160 | bytes 16777216 | tf_op jit(solution)/shard_map/kz,mxyz->mxyk/dot_general | solution.py:45
  149.8 67.7 %fusion.139 = f32[32,64,64,16]{2,3,1,0:T(8,128)} fusion(bf16[32,64,64,16]{2,3,1,0:T(8,128)(2,1)} %subtract_convert_fusion.6, bf16[32,64,64,16]{2,3,1,0:T(8,128)(2,1)} %add_convert_fusion.6, f32[]{:T(128)S(6)} %mul.589, f32[32,16]{1,0:T(8,128)S(1)} %broadcast_multiply_fusion, f32[32,64,64]{2,1,0:T(8,128)S(1)} %broadcast_add_fusion), kind=kOutput, calls=%fused_computation.130 | convolution fusion | flops 83889920 | bytes 17303556 | tf_op jit(solution)/shard_map/kz,mxyz->mxyk/dot_general | solution.py:45
  217.5 64.7 %fusion.137 = f32[32,64,64,16]{2,3,1,0:T(8,128)S(1)} fusion(bf16[32,64,64,16]{2,3,1,0:T(8,128)(2,1)S(1)} %copy-done.2, bf16[32,64,64,16]{2,3,1,0:T(8,128)(2,1)} %add_convert_fusion.6, f32[]{:T(128)S(6)} %mul.589, f32[32,16]{1,0:T(8,128)S(1)} %broadcast_multiply_fusion, f32[32,64,64]{2,1,0:T(8,128)S(1)} %broadcast_add_fusion), kind=kOutput, calls=%fused_computation.129 | convolution fusion | flops 83889920 | bytes 17303556 | tf_op jit(solution)/shard_map/kz,mxyz->mxyk/dot_general | solution.py:45
  282.3 67.8 %add_convert_fusion.5 = bf16[32,64,64,16]{2,3,1,0:T(8,128)(2,1)} fusion(f32[32,64,64,16]{2,3,1,0:T(8,128)} %fusion.139, bf16[32,64,64,16]{2,3,1,0:T(8,128)(2,1)S(1)} %copy-done.2, bf16[32,64,64,16]{2,3,1,0:T(8,128)(2,1)S(1)} %bitcast.174, f32[]{:T(128)S(6)} %mul.589, f32[32,16]{1,0:T(8,128)S(1)} %broadcast_multiply_fusion, ...), kind=kOutput, calls=%fused_computation.31 | convolution fusion | flops 88084224 | bytes 21497860 | tf_op jit(solution)/shard_map/kz,mxyz->mxyk/dot_general | solution.py:45
  350.0 64.5 %subtract_convert_fusion.5 = bf16[32,64,64,16]{2,3,1,0:T(8,128)(2,1)S(1)} fusion(f32[32,64,64,16]{2,3,1,0:T(8,128)S(1)} %fusion.137, bf16[32,64,64,16]{2,3,1,0:T(8,128)(2,1)S(1)} %copy-done.2, bf16[32,64,64,16]{2,3,1,0:T(8,128)(2,1)S(1)} %bitcast.174, f32[]{:T(128)S(6)} %mul.589, f32[32,16]{1,0:T(8,128)S(1)} %broadcast_multiply_fusion, ...), kind=kOutput, calls=%fused_computation.32 | convolution fusion | flops 88084224 | bytes 21497860 | tf_op jit(solution)/shard_map/kz,mxyz->mxyk/dot_general | solution.py:45
  434.5 17.1 %fusion.22 = f32[32,64,16,64]{3,1,2,0:T(8,128)} fusion(f32[32,64,16,64]{3,1,2,0:T(8,128)} %fusion.46, bf16[32,64,64,16]{2,3,1,0:T(8,128)(2,1)} %add_convert_fusion.5), kind=kOutput, calls=%fused_computation.51 | convolution fusion | flops 541188096 | bytes 20971520 | tf_op jit(solution)/shard_map/kx,mxyz->mkyz/dot_general | solution.py:45
  452.0 19.3 %fusion.9 = bf16[32,64,64,16]{1,2,3,0:T(8,128)(2,1)} fusion(f32[32,64,16,64]{3,1,2,0:T(8,128)} %fusion.22, f32[64,64,16]{0,1,2:T(8,128)S(1)} %copy.184, f32[32,64,16,64]{3,1,2,0:T(8,128)} %fusion.42, bf16[32,64,64,16]{2,3,1,0:T(8,128)(2,1)} %copy-done.4), kind=kOutput, calls=%fused_computation.19 | convolution fusion | flops 547479552 | bytes 25427968 | tf_op jit(solution)/shard_map/kx,mxyz->mkyz/dot_general | solution.py:45
  471.3 23.1 %copy.185 = bf16[32,64,64,16]{1,3,2,0:T(8,128)(2,1)} copy(bf16[32,64,64,16]{1,2,3,0:T(8,128)(2,1)} %fusion.9) | data formatting | bytes 8388608 | tf_op jit(solution)/shard_map/convert_element_type | solution.py:73
  504.4 98.2 %all_to_all.60 = bf16[32,64,1024]{2,0,1:T(8,128)(2,1)S(1)} all-to-all(bf16[32,64,1024]{2,0,1:T(8,128)(2,1)} %copy.186), channel_id=1, replica_groups=mesh['dir'=2,'shard'=16] {'shard'}, dimensions={1} | all-to-all | bytes 8388608 | tf_op jit(solution)/shard_map/all_to_all | solution.py:125
  627.4 97.8 %all_to_all.61 = bf16[512,4,1024]{2,1,0:T(4,128)(2,1)S(1)} all-to-all(bf16[512,4,1024]{2,1,0:T(4,128)(2,1)} %copy.188), channel_id=1, replica_groups=mesh['dir'=2,'shard'=16] {'shard'}, dimensions={0} | all-to-all | bytes 8388608 | tf_op jit(solution)/shard_map/all_to_all | solution.py:116
  728.5 14.4 %copy.190 = bf16[32,16,4,1024]{0,3,2,1:T(8,128)(2,1)} copy(bf16[32,16,4,1024]{3,0,1,2:T(8,128)(2,1)} %bitcast.181) | data formatting | bytes 8388608 | tf_op jit(solution)/shard_map/all_to_all | solution.py:116
  742.9 27.9 %copy.191 = bf16[32,64,64,16]{1,2,3,0:T(8,128)(2,1)} copy(bf16[32,64,64,16]{0,3,2,1:T(8,128)(2,1)} %bitcast.177) | data formatting | bytes 8388608 | tf_op jit(solution)/shard_map/reshape | solution.py:60
  808.0 13.9 fusion.63
  821.9 14.2 fusion.37
  836.2 13.9 fusion.60
  850.1 14.4 %fusion.39 = f32[32,64,64,16]{2,3,1,0:T(8,128)} fusion(bf16[32,64,64,16]{2,1,3,0:T(8,128)(2,1)} %fusion.60), kind=kOutput, calls=%fused_computation.68 | convolution fusion | flops 67112704 | bytes 12582912 | tf_op jit(solution)/shard_map/kz,mxyz->mxyk/dot_general | solution.py:45
  864.5 18.4 %add_convert_fusion.2 = bf16[32,64,64,16]{2,3,1,0:T(8,128)(2,1)} fusion(f32[32,64,64,16]{2,3,1,0:T(8,128)} %fusion.37, bf16[32,64,64,16]{2,1,3,0:T(8,128)(2,1)} %fusion.60), kind=kOutput, calls=%fused_computation.24 | convolution fusion | flops 73404160 | bytes 16777216 | tf_op jit(solution)/shard_map/kz,mxyz->mxyk/dot_general | solution.py:45
  883.0 19.1 %subtract_convert_fusion.2 = bf16[32,64,64,16]{2,3,1,0:T(8,128)(2,1)} fusion(f32[32,64,64,16]{2,3,1,0:T(8,128)} %fusion.39, bf16[32,64,64,16]{2,1,3,0:T(8,128)(2,1)} %fusion.63), kind=kOutput, calls=%fused_computation.25 | convolution fusion | flops 73404160 | bytes 16777216 | tf_op jit(solution)/shard_map/kz,mxyz->mxyk/dot_general | solution.py:45
  902.1 67.5 %fusion.145 = f32[32,64,64,16]{2,3,1,0:T(8,128)} fusion(bf16[32,64,64,16]{2,3,1,0:T(8,128)(2,1)} %subtract_convert_fusion.2, bf16[32,64,64,16]{2,3,1,0:T(8,128)(2,1)} %add_convert_fusion.2, f32[]{:T(128)S(6)} %mul.589, f32[32,16]{1,0:T(8,128)S(1)} %copy-done.13, f32[32,64,64]{2,1,0:T(8,128)S(1)} %copy-done.9), kind=kOutput, calls=%fused_computation.132 | convolution fusion | flops 83889920 | bytes 17303556 | tf_op jit(solution)/shard_map/kz,mxyz->mxyk/dot_general | solution.py:45
  969.6 62.7 %fusion.143 = f32[32,64,64,16]{2,3,1,0:T(8,128)S(1)} fusion(bf16[32,64,64,16]{2,3,1,0:T(8,128)(2,1)S(1)} %copy-done.3, bf16[32,64,64,16]{2,3,1,0:T(8,128)(2,1)S(1)} %bitcast.176, f32[]{:T(128)S(6)} %mul.589, f32[32,16]{1,0:T(8,128)S(1)} %copy-done.13, f32[32,64,64]{2,1,0:T(8,128)S(1)} %copy-done.9), kind=kOutput, calls=%fused_computation.131 | convolution fusion | flops 83889920 | bytes 17303556 | tf_op jit(solution)/shard_map/kz,mxyz->mxyk/dot_general | solution.py:45
  1032.4 67.8 %add_convert_fusion.1 = bf16[32,64,64,16]{2,3,1,0:T(8,128)(2,1)} fusion(f32[32,64,64,16]{2,3,1,0:T(8,128)} %fusion.145, bf16[32,64,64,16]{2,3,1,0:T(8,128)(2,1)S(1)} %copy-done.3, bf16[32,64,64,16]{2,3,1,0:T(8,128)(2,1)S(1)} %bitcast.176, f32[]{:T(128)S(6)} %mul.589, f32[32,16]{1,0:T(8,128)S(1)} %copy-done.13, f32[32,64,64]{2,1,0:T(8,128)S(1)} %copy-done.9), kind=kOutput, calls=%fused_computation.22 | convolution fusion | flops 88084224 | bytes 21497860 | tf_op jit(solution)/shard_map/kz,mxyz->mxyk/dot_general | solution.py:45
  1100.1 66.7 %subtract_convert_fusion.1 = bf16[32,64,64,16]{2,3,1,0:T(8,128)(2,1)} fusion(f32[32,64,64,16]{2,3,1,0:T(8,128)S(1)} %fusion.143, bf16[32,64,64,16]{2,3,1,0:T(8,128)(2,1)S(1)} %copy-done.3, bf16[32,64,64,16]{2,3,1,0:T(8,128)(2,1)S(1)} %bitcast.176, f32[]{:T(128)S(6)} %mul.589, f32[32,16]{1,0:T(8,128)S(1)} %copy-done.13, f32[32,64,64]{2,1,0:T(8,128)S(1)} %copy-done.9), kind=kOutput, calls=%fused_computation.23 | convolution fusion | flops 88084224 | bytes 21497860 | tf_op jit(solution)/shard_map/kz,mxyz->mxyk/dot_general | solution.py:45
  1185.7 17.1 %fusion.13 = f32[32,64,16,64]{3,1,2,0:T(8,128)} fusion(f32[32,64,16,64]{3,1,2,0:T(8,128)} %fusion.34, bf16[32,64,64,16]{2,3,1,0:T(8,128)(2,1)} %add_convert_fusion.1), kind=kOutput, calls=%fused_computation.42 | convolution fusion | flops 541188096 | bytes 20971520 | tf_op jit(solution)/shard_map/kx,mxyz->mkyz/dot_general | solution.py:45
  1202.7 18.9 %fusion.8 = bf16[32,64,64,16]{1,2,3,0:T(8,128)(2,1)} fusion(f32[32,64,16,64]{3,1,2,0:T(8,128)} %fusion.13, f32[64,64,16]{0,1,2:T(8,128)S(1)} %copy-done.11, f32[32,64,16,64]{3,1,2,0:T(8,128)} %fusion.30, bf16[32,64,64,16]{2,3,1,0:T(8,128)(2,1)} %subtract_convert_fusion.1), kind=kOutput, calls=%fused_computation.17 | convolution fusion | flops 547479552 | bytes 25427968 | tf_op jit(solution)/shard_map/kx,mxyz->mkyz/dot_general | solution.py:45
  1221.6 23.3 %copy.207 = bf16[32,64,64,16]{1,3,2,0:T(8,128)(2,1)} copy(bf16[32,64,64,16]{1,2,3,0:T(8,128)(2,1)} %fusion.8) | data formatting | bytes 8388608 | tf_op jit(solution)/shard_map/convert_element_type | solution.py:73
  1255.0 97.4 %all_to_all.62 = bf16[32,64,1024]{2,0,1:T(8,128)(2,1)S(1)} all-to-all(bf16[32,64,1024]{2,0,1:T(8,128)(2,1)} %copy.208), channel_id=1, replica_groups=mesh['dir'=2,'shard'=16] {'shard'}, dimensions={1} | all-to-all | bytes 8388608 | tf_op jit(solution)/shard_map/all_to_all | solution.py:125
  1382.6 45.1 %all-to-all-done.3 = bf16[1,512,4,1024]{1,2,0,3:T(4,128)(2,1)} async-done(((bf16[1,512,4,1024]{1,2,0,3:T(4,128)(2,1)}), bf16[1,512,4,1024]{1,2,0,3:T(4,128)(2,1)}, u32[]{:S(2)}, u32[]{:S(2)}) %all-to-all-start.3) | async-done | bytes 4194336 | tf_op jit(solution)/shard_map/all_to_all | solution.py:127
  (98 shorter events, 219.5 us)
Async XLA Ops:
  0.6 609.9 %copy-start = (bf16[512,441]{0,1:T(8,128)(2,1)S(1)}, bf16[512,441]{0,1:T(8,128)(2,1)}, u32[]{:S(2)}) copy-start(bf16[512,441]{0,1:T(8,128)(2,1)} %param.12) | copy-start | bytes 1354756
  21.8 9.2 copy-start.7
  37.5 11.7 copy-start.6
  149.8 200.3 %copy-start.8 = (f32[32,64,64]{2,1,0:T(8,128)}, f32[32,64,64]{2,1,0:T(8,128)S(1)}, u32[]{:S(2)}) copy-start(f32[32,64,64]{2,1,0:T(8,128)S(1)} %broadcast_add_fusion) | copy-start | bytes 1572868
  149.8 200.2 %copy-start.12 = (f32[32,16]{1,0:T(8,128)}, f32[32,16]{1,0:T(8,128)S(1)}, u32[]{:S(2)}) copy-start(f32[32,16]{1,0:T(8,128)S(1)} %broadcast_multiply_fusion) | copy-start | bytes 6148
  149.8 67.7 %copy-start.2 = (bf16[32,64,64,16]{2,3,1,0:T(8,128)(2,1)S(1)}, bf16[32,64,64,16]{2,3,1,0:T(8,128)(2,1)}, u32[]{:S(2)}) copy-start(bf16[32,64,64,16]{2,3,1,0:T(8,128)(2,1)} %subtract_convert_fusion.6) | copy-start | bytes 12582916
  149.8 132.4 %slice-start = ((s8[8388608]{0:T(1024)(128)(4,1)}), s8[4194304]{0:T(1024)(128)(4,1)S(1)}, s32[]{:S(2)}) async-start(s8[8388608]{0:T(1024)(128)(4,1)} %bitcast.173), calls=%async_computation.4 | async-start | bytes 8388608
  217.5 64.7 %slice-start.1 = ((s8[8388608]{0:T(1024)(128)(4,1)}), s8[4194304]{0:T(1024)(128)(4,1)S(1)}, s32[]{:S(2)}) async-start(s8[8388608]{0:T(1024)(128)(4,1)} %bitcast.173), calls=%async_computation.5 | async-start | bytes 8388608
  414.5 8.3 copy-start.4
  434.5 17.1 %copy-start.14 = (f32[64,1024]{1,0:T(8,128)S(1)}, f32[64,1024]{1,0:T(8,128)}, u32[]{:S(2)}) copy-start(f32[64,1024]{1,0:T(8,128)} %param.8) | copy-start | bytes 786436
  452.0 19.3 %copy-start.10 = (f32[64,64,16]{0,1,2:T(8,128)}, f32[64,64,16]{0,1,2:T(8,128)S(1)}, u32[]{:S(2)}) copy-start(f32[64,64,16]{0,1,2:T(8,128)S(1)} %copy.184) | copy-start | bytes 786436
  602.6 7.9 copy-start.17
  602.6 7.9 copy-start.19
  789.0 11.8 copy-start.1
  883.0 19.1 %copy-start.9 = (f32[32,64,64]{2,1,0:T(8,128)S(1)}, f32[32,64,64]{2,1,0:T(8,128)}, u32[]{:S(2)}) copy-start(f32[32,64,64]{2,1,0:T(8,128)} %copy-done.8) | copy-start | bytes 1572868
  883.0 19.1 %copy-start.13 = (f32[32,16]{1,0:T(8,128)S(1)}, f32[32,16]{1,0:T(8,128)}, u32[]{:S(2)}) copy-start(f32[32,16]{1,0:T(8,128)} %copy-done.12) | copy-start | bytes 6148
  883.0 86.7 %slice-start.2 = ((s8[8388608]{0:T(1024)(128)(4,1)}), s8[4194304]{0:T(1024)(128)(4,1)S(1)}, s32[]{:S(2)}) async-start(s8[8388608]{0:T(1024)(128)(4,1)} %bitcast.175), calls=%async_computation.6 | async-start | bytes 8388608
  902.1 67.5 %slice-start.3 = ((s8[8388608]{0:T(1024)(128)(4,1)}), s8[4194304]{0:T(1024)(128)(4,1)S(1)}, s32[]{:S(2)}) async-start(s8[8388608]{0:T(1024)(128)(4,1)} %bitcast.175), calls=%async_computation.7 | async-start | bytes 8388608
  902.1 67.5 %copy-start.3 = (bf16[32,64,64,16]{2,3,1,0:T(8,128)(2,1)S(1)}, bf16[32,64,64,16]{2,3,1,0:T(8,128)(2,1)}, u32[]{:S(2)}) copy-start(bf16[32,64,64,16]{2,3,1,0:T(8,128)(2,1)} %subtract_convert_fusion.2) | copy-start | bytes 12582916
  1166.8 11.7 copy-start.5
  1185.7 17.1 %copy-start.11 = (f32[64,64,16]{0,1,2:T(8,128)S(1)}, f32[64,64,16]{0,1,2:T(8,128)}, u32[]{:S(2)}) copy-start(f32[64,64,16]{0,1,2:T(8,128)} %copy-done.10) | copy-start | bytes 786436
  1352.4 7.9 copy-start.18
  1352.4 7.9 copy-start.20
  1369.1 13.5 copy-start.15
  1376.7 51.0 %all-to-all-start.3 = ((bf16[1,512,4,1024]{1,2,0,3:T(4,128)(2,1)}), bf16[1,512,4,1024]{1,2,0,3:T(4,128)(2,1)}, u32[]{:S(2)}, u32[]{:S(2)}) async-start(bf16[1,512,4,1024]{1,2,0,3:T(4,128)(2,1)} %copy.210), calls=%async_computation.3 | async-start | bytes 8388608 | tf_op jit(solution)/shard_map/all_to_all | solution.py:127
  1382.6 48.8 %copy-start.16 = (f32[512]{0:T(512)S(1)}, f32[512]{0:T(512)}, u32[]{:S(2)}) copy-start(f32[512]{0:T(512)} %param.10) | copy-start | bytes 6148
where the time goes:
time: 1450 us; the launch traced here: 1440 us
  matrix products  919 us (63%)
  blocking collectives  293 us (20%)
  local copies, waits for them, and re-layouts  171 us (12%)
  waiting for transfers between devices  45.1 us (3%)
    dot_general x36, matrix products, along_axis(): jnp.einsum(patterns[position], table, values, preferred_element_type=jnp....  898 us
    all_to_all x2, blocking collectives, on_device(): lax.all_to_all(moved, 'shard', split_axis=1, concat_axis=0, tiled=True)  196 us
    all_to_all x1, blocking collectives, diffuse_back(): lax.all_to_all(diffuse_only(points), 'shard', split_axis=0, concat_axis=1...  97.8 us
    convert_element_type x2, local copies, waits for them, and re-layouts, transport(): (summed * damping[None]).astype(jnp.bfloat16).reshape(flat_values.shape)  46.4 us
    all_to_all x1, waiting for transfers between devices, on_device(): lax.all_to_all(result[None], 'dir', split_axis=3, concat_axis=0, tiled=True)  45.1 us
  transfers between devices with their start and end apart: 1, of which 1 were waited for; matrix products, arithmetic and copies ran while one was open for 0% of the time, Pallas kernels for 0%

commit v1 on v0

v1 whole, which is shorter than its diff:
```python
import functools
import math

import jax
import jax.numpy as jnp
import numpy as np
from jax import lax
from jax.experimental import pallas as pl
from jax.experimental.pallas import tpu as pltpu
from jax.sharding import PartitionSpec as P

NY = 64
STEPS = 2

transport_length = 1.5
one_third = 1.0 / 3.0
VMEM_LIMIT = 60 * 1024 * 1024


def half_spectrum(ny, nz):
    selfs = [(0, 0), (ny // 2, 0), (0, nz // 2), (ny // 2, nz // 2)]
    pairs = []
    for ky in range(ny):
        for kz in range(nz):
            mirror = ((-ky) % ny, (-kz) % nz)
            if (ky, kz) < mirror:
                pairs.append((ky, kz))
    first = selfs[:2] + pairs
    second = selfs[2:] + pairs
    return np.array(first + second, np.int64)


def real_basis(ny, nz):
    freq = half_spectrum(ny, nz)
    half = len(freq) // 2
    y = np.repeat(np.arange(ny), nz)[:, None]
    z = np.tile(np.arange(nz), ny)[:, None]
    angle = 2.0 * np.pi * (y * freq[None, :, 0] / ny + z * freq[None, :, 1] / nz)
    basis = np.cos(angle)
    basis[:, half + 2 :] = -np.sin(angle[:, half + 2 :])
    return basis


def signed(k, length):
    return np.where(k <= (length - 1) // 2, k, k - length) * (2.0 * np.pi / length)


def plane_tables(heading, scale, ny, nz):
    freq = half_spectrum(ny, nz)
    lanes = len(freq)
    half = lanes // 2
    wave_y = jnp.asarray(signed(freq[:, 0], ny), jnp.float32)
    wave_z = jnp.asarray(signed(freq[:, 1], nz), jnp.float32)
    theta_y = scale * heading[1][:, None] * wave_y[None, :]
    theta_z = scale * heading[2][:, None] * wave_z[None, :]
    cy, sy, cz, sz = jnp.cos(theta_y), jnp.sin(theta_y), jnp.cos(theta_z), jnp.sin(theta_z)
    ny_mask = freq[:, 0] == ny // 2
    nz_mask = freq[:, 1] == nz // 2
    only_y = jnp.asarray(ny_mask & ~nz_mask)[None]
    only_z = jnp.asarray(nz_mask & ~ny_mask)[None]
    both = jnp.asarray(ny_mask & nz_mask)[None]
    cos_sum = cy * cz - sy * sz
    sin_sum = sy * cz + cy * sz
    single = only_y | only_z
    cu = jnp.where(single, cy * cz, cos_sum)
    su = jnp.where(only_z, sy * cz, jnp.where(only_y, sz * cy, jnp.where(both, 0.0, sin_sum)))
    cv = jnp.where(
        only_z, -cy * sz, jnp.where(only_y, -cz * sy, jnp.where(both, -sin_sum, 0.0))
    )
    sv = jnp.where(single, -sy * sz, 0.0)
    weight = np.full((lanes,), 2.0 / (ny * nz))
    weight[[0, 1, half, half + 1]] = 1.0 / (ny * nz)
    turn = np.where(np.arange(lanes) < half, 1.0, -1.0)
    weight = jnp.asarray(weight, jnp.float32)[None]
    turn = jnp.asarray(turn, jnp.float32)[None]
    return cu * weight, su * weight * turn, cv * weight, sv * weight * turn


def line_operator(heading, scale, nx, group):
    count = heading.shape[1]
    k = np.arange(1, nx // 2)
    theta = scale * heading[0][:, None] * jnp.asarray(k * (2.0 * np.pi / nx), jnp.float32)[None]
    theta_n = -scale * heading[0][:, None] * math.pi
    trig = jnp.concatenate(
        [jnp.ones((count, 1), jnp.float32), jnp.cos(theta), jnp.sin(theta), jnp.cos(theta_n)], 1
    )
    gap = (np.arange(nx)[:, None] - np.arange(nx)[None, :]) % nx
    angle = 2.0 * np.pi * ((k[:, None, None] * gap[None]) % nx) / nx
    rows = np.concatenate(
        [np.ones((1, nx, nx)), 2 * np.cos(angle), 2 * np.sin(angle), (1.0 - 2.0 * (gap % 2))[None]]
    )
    table = jnp.asarray(rows / nx, jnp.float32)
    operator = jnp.einsum("gmk,kax->gamx", trig.reshape(-1, group, nx), table,
                          precision=lax.Precision.HIGHEST)
    operator = operator.reshape(count // group, nx * group, nx)
    sign = jnp.asarray(1.0 - 2.0 * (np.arange(nx) % 2), jnp.float32)
    extra = jnp.broadcast_to(sign, (count // group, group, nx))
    operator = jnp.concatenate([operator, extra], 1).astype(jnp.bfloat16)
    return operator, jnp.sin(theta_n) / nx


def to_rows(block):
    a, b, lanes = block.shape
    if b % 16:
        return block.astype(jnp.float32).reshape(a * b, lanes).astype(jnp.bfloat16)
    return block.reshape(a * b, lanes)


def swap(values):
    half = values.shape[-1] // 2
    return jnp.concatenate([values[..., half:], values[..., :half]], axis=-1)


def transport_kernel(by_cell, group, nx, halves, q_ref, p_ref, c_ref, s_ref, cv_ref, sv_ref,
                     w_ref, damping_ref, out_ref, z_ref, l_ref):
    rows = nx * group
    lanes = w_ref.shape[1]
    width = lanes // halves
    col = lax.broadcasted_iota(jnp.int32, (nx, rows), 1)
    line = lax.broadcasted_iota(jnp.int32, (nx, rows), 0)
    col_x = col // group if by_cell else col % nx
    expand = jnp.where(col_x == line, 1.0, 0.0).astype(jnp.bfloat16)
    wide = jnp.dot(p_ref[0], expand, preferred_element_type=jnp.float32)
    row_at = lax.broadcasted_iota(jnp.int32, wide.shape, 0)
    col_at = lax.broadcasted_iota(jnp.int32, wide.shape, 1)
    col_m = col_at % group if by_cell else col_at // nx
    l_ref[...] = jnp.where(row_at % group == col_m, wide, 0.0).astype(jnp.bfloat16)

    outer = q_ref.shape[0]
    chunks = 4
    part = outer // chunks
    step_rows = rows // chunks

    def forward(i, carry):
        block = to_rows(q_ref[pl.ds(i * part, part)])
        z = jnp.dot(block, w_ref[...], preferred_element_type=jnp.float32)
        start = pl.multiple_of(i * step_rows, step_rows)
        z_ref[pl.ds(start, step_rows), :] = z.astype(jnp.bfloat16)
        return carry

    lax.fori_loop(0, chunks, forward, 0)

    ripple = jnp.dot(l_ref[rows:, :], z_ref[...], preferred_element_type=jnp.float32)
    cross = ripple * cv_ref[...] + swap(ripple) * sv_ref[...]
    part_x = nx // chunks

    def backward(i, carry):
        start = pl.multiple_of(i * step_rows, step_rows)
        y = jnp.dot(l_ref[pl.ds(start, step_rows), :], z_ref[...],
                    preferred_element_type=jnp.float32)
        y = y.reshape(part_x, group, lanes)
        odd = lax.broadcasted_iota(jnp.int32, y.shape, 0) % 2 == 1
        turned = y * c_ref[...][None] + swap(y) * s_ref[...][None]
        turned = turned + jnp.where(odd, -cross[None], cross[None])
        turned = turned.reshape(step_rows, lanes).astype(jnp.bfloat16)
        back = lax.dot_general(turned, w_ref[...], (((1,), (1,)), ((), ())),
                               preferred_element_type=jnp.float32)
        x_at = pl.multiple_of(i * part_x, part_x)
        back = back.reshape(part_x, group, lanes) * damping_ref[pl.ds(x_at, part_x), :][:, None, :]
        back = back.astype(jnp.bfloat16)
        for h in range(halves):
            out_ref[h, pl.ds(x_at, part_x)] = back[:, :, h * width : (h + 1) * width]
        return carry

    lax.fori_loop(0, chunks, backward, 0)


def transport(q, by_cell, halves, operator, tables, basis, damping):
    nx, lanes = damping.shape
    count = q.shape[1] if by_cell else q.shape[0]
    group = operator.shape[1] // (nx + 1)
    rows = nx * group


    if by_cell:
        q_spec = pl.BlockSpec((nx, group, lanes), lambda g: (0, g, 0))
    else:
        q_spec = pl.BlockSpec((group, nx, lanes), lambda g: (g, 0, 0))
    table_spec = pl.BlockSpec((group, lanes), lambda g: (g, 0))
    return pl.pallas_call(
        functools.partial(transport_kernel, by_cell, group, nx, halves),
        out_shape=jax.ShapeDtypeStruct((halves, nx, count, lanes // halves), jnp.bfloat16),
        grid=(count // group,),
        in_specs=[
            q_spec,
            pl.BlockSpec((1, rows + group, nx), lambda g: (g, 0, 0)),
            table_spec, table_spec, table_spec, table_spec,
            pl.BlockSpec((lanes, lanes), lambda g: (0, 0)),
            pl.BlockSpec((nx, lanes), lambda g: (0, 0)),
        ],
        out_specs=pl.BlockSpec((halves, nx, group, lanes // halves), lambda g: (0, 0, g, 0)),
        scratch_shapes=[
            pltpu.VMEM((rows, lanes), jnp.bfloat16),
            pltpu.VMEM((rows + group, rows), jnp.bfloat16),
        ],
        compiler_params=pltpu.CompilerParams(vmem_limit_bytes=VMEM_LIMIT),
    )(q, operator, *tables, basis, damping)


def mix(block, analysis_ref, synthesis_ref, decay_ref):
    harmonic = jnp.dot(analysis_ref[...], block, preferred_element_type=jnp.float32)
    harmonic = (harmonic * decay_ref[...]).astype(jnp.bfloat16)
    return jnp.dot(synthesis_ref[...], harmonic, preferred_element_type=jnp.float32)


def diffuse_kernel(points_ref, analysis_ref, synthesis_ref, decay_ref, out_ref):
    n, _, count, width = points_ref.shape
    block = to_rows(points_ref[:, 0])
    mixed = mix(block, analysis_ref, synthesis_ref, decay_ref)
    out_ref[:, 0] = mixed.reshape(n, count, width).astype(jnp.bfloat16)


def diffuse(points, analysis, synthesis, decay):
    n, rows, count, lanes = points.shape
    width = lanes // 2
    spec = pl.BlockSpec((n, 1, count, width), lambda i, j: (0, i, 0, j))
    whole = pl.BlockSpec(analysis.shape, lambda i, j: (0, 0))
    return pl.pallas_call(
        diffuse_kernel,
        out_shape=jax.ShapeDtypeStruct(points.shape, jnp.bfloat16),
        grid=(rows, 2),
        in_specs=[
            spec,
            whole,
            pl.BlockSpec(synthesis.shape, lambda i, j: (0, 0)),
            pl.BlockSpec(decay.shape, lambda i, j: (0, 0)),
        ],
        out_specs=spec,
        compiler_params=pltpu.CompilerParams(vmem_limit_bytes=VMEM_LIMIT),
    )(points, analysis, synthesis, decay)


def moment_kernel(points_ref, analysis_ref, synthesis_ref, decay_ref, table_ref, out_ref):
    product = None
    for p in range(2):
        block = to_rows(points_ref[p, :, 0])
        mixed = mix(block, analysis_ref, synthesis_ref, decay_ref)
        mixed = mixed.astype(jnp.bfloat16).astype(jnp.float32)
        product = mixed if product is None else product * mixed
    out_ref[0] = jnp.dot(table_ref[...], product, precision=lax.Precision.HIGHEST,
                         preferred_element_type=jnp.float32)


def moments(points, analysis, synthesis, decay, table):
    two, n, rows, count, width = points.shape
    return pl.pallas_call(
        moment_kernel,
        out_shape=jax.ShapeDtypeStruct((rows, table.shape[0], width), jnp.float32),
        grid=(rows,),
        in_specs=[
            pl.BlockSpec((two, n, 1, count, width), lambda i: (0, 0, i, 0, 0)),
            pl.BlockSpec(analysis.shape, lambda i: (0, 0)),
            pl.BlockSpec(synthesis.shape, lambda i: (0, 0)),
            pl.BlockSpec(decay.shape, lambda i: (0, 0)),
            pl.BlockSpec(table.shape, lambda i: (0, 0)),
        ],
        out_specs=pl.BlockSpec((1, table.shape[0], width), lambda i: (i, 0, 0)),
        compiler_params=pltpu.CompilerParams(vmem_limit_bytes=VMEM_LIMIT),
    )(points, analysis, synthesis, decay, table)


def moment_table(orient, quad_weights):
    head_x, head_y, head_z = (orient[0], orient[1], orient[2])
    unity = jnp.ones_like(head_x)
    zero = jnp.zeros_like(head_x)
    moment_rows = [
        unity,
        head_x * head_x - one_third,
        head_y * head_y - one_third,
        head_x * head_y,
        head_x * head_z,
        head_y * head_z,
        zero,
        zero,
    ]
    return jnp.stack(moment_rows) * quad_weights[None, :]


def on_device(propagators, field, orient, quad_weights, analysis, synthesis, decay):
    state = propagators[0]
    count, nx, lanes = state.shape
    nz = lanes // NY
    shards = lax.axis_size("shard")
    group = min(16, count)
    offset = lax.axis_index("shard") * count
    heading = lax.dynamic_slice_in_dim(orient, offset, count, 1)
    direction = 1.0 - 2.0 * lax.axis_index("dir").astype(jnp.float32)
    scale = direction * transport_length
    operator, nyquist = line_operator(heading, scale, nx, group)
    cu, su, cv, sv = plane_tables(heading, scale, NY, nz)
    tables = (cu, su, cv * nyquist, sv * nyquist)
    basis = jnp.asarray(real_basis(NY, nz).astype(jnp.bfloat16))
    damping = jnp.exp(-field)
    harmonics, total = analysis.shape
    pad = -harmonics % 128
    analysis = jnp.pad(analysis, ((0, pad), (0, 0)))
    synthesis = jnp.pad(synthesis, ((0, 0), (0, pad)))
    decay = jnp.pad(decay, (0, pad))[:, None]

    by_cell = False
    for contour in range(STEPS):
        is_last = contour == STEPS - 1
        halves = lax.axis_size("dir") if is_last else 1
        moved = transport(state, by_cell, halves, operator, tables, basis, damping)
        if is_last:
            moved = moved.reshape(halves * shards, nx // shards, count, lanes // halves)
            moved = lax.all_to_all(moved, ("dir", "shard"), 0, 0, tiled=True)
            moved = moved.reshape(halves, shards, nx // shards, count, lanes // halves)
            table = moment_table(orient, quad_weights)
            result = moments(moved, analysis, synthesis, decay, table)
        else:
            moved = moved.reshape(shards, nx // shards, count, lanes)
            moved = lax.all_to_all(moved, "shard", 0, 0, tiled=True)
            mixed = diffuse(moved, analysis, synthesis, decay)
            mixed = lax.all_to_all(mixed, "shard", 0, 0, tiled=True)
            state = mixed.reshape(nx, count, lanes)
            by_cell = True
    return result[:, 0], jnp.moveaxis(result[:, 1:6], 1, 0)


def solution(mesh):
    in_specs = (P("dir", "shard", None, None), P(), P(), P(), P(), P(), P())
    out_specs = (P("shard", "dir"), P(None, "shard", "dir"))
    return jax.shard_map(
        on_device, mesh=mesh, in_specs=in_specs, out_specs=out_specs, check_vma=False
    )
```

time: 1450 us -> 377 us (0.26)
  matrix products: 919 us -> 2.72 us
  blocking collectives: 293 us -> 97 us
  local copies, waits for them, and re-layouts: 171 us -> 6.79 us
  waiting for transfers between devices: 45.1 us -> 181 us
  Pallas kernels: 0 us -> 66.5 us
    dot_general x39 -> x1, matrix products: 919 us -> 2.72 us  [line_operator(): jnp.einsum('gmk,kax->gamx', trig.reshape(-1, group, nx), table, precision...]
    all_to_all x3 -> x1, blocking collectives: 293 us -> 97 us  [on_device(): mixed = lax.all_to_all(mixed, 'shard', 0, 0, tiled=True)]
    all_to_all x1 -> x2, waiting for transfers between devices: 45.1 us -> 181 us  [the longest x1 91.6 us: on_device(): moved = lax.all_to_all(moved, ('dir', 'shard'), 0, 0, tiled=True)]
    pallas_call x0 -> x4, Pallas kernels: none -> 66.5 us  [the longest x2 46.3 us: transport(): pl.pallas_call(functools.partial(transport_kernel, by_cell, group, nx, ha...]
    reshape x5 -> x0, local copies, waits for them, and re-layouts: 56.8 us -> none  [the longest x1 27.9 us: transport(): values = flat_values.reshape(flat_values.shape[0], NX, NY, NZ)]
    convert_element_type x2 -> x0, local copies, waits for them, and re-layouts: 46.4 us -> none  [transport(): (summed * damping[None]).astype(jnp.bfloat16).reshape(flat_values.shape)]
    all_to_all x5 -> x0, local copies, waits for them, and re-layouts: 27.9 us -> none  [the longest x2 17.7 us: diffuse_back(): lax.all_to_all(diffuse_only(points), 'shard', split_axis=0, concat_axis=1...]
    another operation x3 -> x0, local copies, waits for them, and re-layouts: 20.9 us -> none  [the longest x1 12.7 us: transport(): values = flat_values.reshape(flat_values.shape[0], NX, NY, NZ)]
  transfers between devices with their start and end apart: 1 -> 2, of which waited for: 1 -> 2; matrix products, arithmetic and copies ran while one was open for 0% -> 1% of each run, Pallas kernels for 0% -> 0%
where the time goes in v1:
time: 377 us; the launch traced here: 373 us
  waiting for transfers between devices  181 us (48%)
  blocking collectives  97 us (26%)
  Pallas kernels  66.5 us (18%)
  starting transfers between devices  12.1 us (3%)
  local copies, waits for them, and re-layouts  6.79 us (2%)
  other arithmetic  6.11 us (2%)
    all_to_all x1, blocking collectives, on_device(): mixed = lax.all_to_all(mixed, 'shard', 0, 0, tiled=True)  97 us
    all_to_all x1, waiting for transfers between devices, on_device(): moved = lax.all_to_all(moved, ('dir', 'shard'), 0, 0, tiled=True)  91.6 us
    all_to_all x1, waiting for transfers between devices, on_device(): moved = lax.all_to_all(moved, 'shard', 0, 0, tiled=True)  89.3 us
    pallas_call x2, Pallas kernels, transport(): pl.pallas_call(functools.partial(transport_kernel, by_cell, group, nx, ha...  46.3 us
    pallas_call x1, Pallas kernels, diffuse(): pl.pallas_call(diffuse_kernel, out_shape=jax.ShapeDtypeStruct(points.shap...  10.1 us
    pallas_call x1, Pallas kernels, moments(): pl.pallas_call(moment_kernel, out_shape=jax.ShapeDtypeStruct((rows, table...  10.1 us
  transfers between devices with their start and end apart: 2, of which 2 were waited for; matrix products, arithmetic and copies ran while one was open for 1% of the time, Pallas kernels for 0%

profile of v1, /device:TPU:19, one launch (start us, length us, event | category | flops | bytes accessed | tf_op | source)
XLA Modules:
  0.0 372.9 jit_solution(16039684690066380617)
XLA Ops:
  0.6 0.0 copy-start.13
  0.7 0.8 constant_dynamic-slice_fusion
  1.4 0.1 multiply_bitcast_fusion
  1.5 0.1 mul.237
  1.6 0.1 cos.30
  1.7 0.0 copy-start.3
  1.7 0.0 copy-start.5
  1.7 0.0 copy-start.6
  1.7 0.0 copy-start.9
  1.8 1.7 negate_exponential_fusion.damping_ref
  3.5 0.8 multiply_cosine_fusion.2
  4.3 2.7 convolution_convert_fusion
  7.1 0.9 pad_maximum_fusion.p_ref
  8.1 1.9 fusion.23
  10.0 23.3 %shard_map.185 = bf16[1,64,32,1024]{3,2,1,0:T(8,128)(2,1)} custom-call(bf16[32,64,1024]{2,1,0:T(8,128)(2,1)} %bitcast.31, bf16[2,1040,64]{2,1,0:T(8,128)(2,1)} %pad_maximum_fusion.p_ref, f32[32,1024]{1,0:T(8,128)} %get-tuple-element.11.c_ref, f32[32,1024]{1,0:T(8,128)} %get-tuple-element.9.s_ref, f32[32,1024]{1,0:T(8,128)} %get-tuple-element.10.cv_ref, ...), custom_call_target="tpu_custom_call" | custom-call | tf_op jit(solution)/shard_map/pallas_call | solution.py:180
  33.3 6.6 %all-to-all-start = ((bf16[16,4,32,1024]{3,2,1,0:T(8,128)(2,1)}), bf16[16,4,32,1024]{3,2,1,0:T(8,128)(2,1)}, u32[]{:S(2)}, u32[]{:S(2)}) async-start(bf16[16,4,32,1024]{3,2,1,0:T(8,128)(2,1)} %bitcast.29), calls=%async_computation | async-start | bytes 8388608 | tf_op jit(solution)/shard_map/all_to_all | solution.py:313
  40.0 0.2 copy.24
  40.2 0.9 pad.13.synthesis_ref
  41.1 0.8 pad.12.analysis_ref
  41.9 0.9 copy.25.decay_ref
  42.8 89.3 %all-to-all-done.points_ref = bf16[16,4,32,1024]{3,2,1,0:T(8,128)(2,1)} async-done(((bf16[16,4,32,1024]{3,2,1,0:T(8,128)(2,1)}), bf16[16,4,32,1024]{3,2,1,0:T(8,128)(2,1)}, u32[]{:S(2)}, u32[]{:S(2)}) %all-to-all-start) | async-done | bytes 4194336 | tf_op jit(solution)/shard_map/all_to_all | solution.py:313
  132.0 10.1 %shard_map.186 = bf16[16,4,32,1024]{3,2,1,0:T(8,128)(2,1)} custom-call(bf16[16,4,32,1024]{3,2,1,0:T(8,128)(2,1)} %all-to-all-done.points_ref, bf16[512,512]{1,0:T(8,128)(2,1)} %pad.12.analysis_ref, bf16[512,512]{1,0:T(8,128)(2,1)} %pad.13.synthesis_ref, f32[512,1]{1,0:T(8,128)} %copy.25.decay_ref), custom_call_target="tpu_custom_call" | custom-call | tf_op jit(solution)/shard_map/pallas_call | solution.py:218
  142.2 97.0 %all_to_all.15 = bf16[16,4,32,1024]{3,2,1,0:T(8,128)(2,1)} all-to-all(bf16[16,4,32,1024]{3,2,1,0:T(8,128)(2,1)} %shard_map.186), channel_id=1, replica_groups=mesh['dir'=2,'shard'=16] {'shard'}, dimensions={0} | all-to-all | bytes 8388608 | tf_op jit(solution)/shard_map/all_to_all | solution.py:315
  239.2 22.9 %shard_map.187 = bf16[2,64,32,512]{3,2,1,0:T(8,128)(2,1)} custom-call(bf16[64,32,1024]{2,1,0:T(8,128)(2,1)} %bitcast.30, bf16[2,1040,64]{2,1,0:T(8,128)(2,1)} %pad_maximum_fusion.p_ref, f32[32,1024]{1,0:T(8,128)} %get-tuple-element.11.c_ref, f32[32,1024]{1,0:T(8,128)} %get-tuple-element.9.s_ref, f32[32,1024]{1,0:T(8,128)} %get-tuple-element.10.cv_ref, ...), custom_call_target="tpu_custom_call" | custom-call | tf_op jit(solution)/shard_map/pallas_call | solution.py:180
  262.1 5.5 %all-to-all-start.2 = ((bf16[32,4,32,512]{3,2,1,0:T(8,128)(2,1)}), bf16[32,4,32,512]{3,2,1,0:T(8,128)(2,1)}, u32[]{:S(2)}, u32[]{:S(2)}) async-start(bf16[32,4,32,512]{3,2,1,0:T(8,128)(2,1)} %bitcast.28), calls=%async_computation.2 | async-start | bytes 8388608 | tf_op jit(solution)/shard_map/all_to_all | solution.py:307
  267.7 0.6 broadcast_multiply_fusion.table_ref
  268.3 91.6 %all-to-all-done.2 = bf16[32,4,32,512]{3,2,1,0:T(8,128)(2,1)} async-done(((bf16[32,4,32,512]{3,2,1,0:T(8,128)(2,1)}), bf16[32,4,32,512]{3,2,1,0:T(8,128)(2,1)}, u32[]{:S(2)}, u32[]{:S(2)}) %all-to-all-start.2) | async-done | bytes 4194336 | tf_op jit(solution)/shard_map/all_to_all | solution.py:307
  359.9 10.1 %shard_map.188 = f32[4,8,512]{2,1,0:T(8,128)} custom-call(bf16[2,16,4,32,512]{4,3,2,1,0:T(8,128)(2,1)} %bitcast.13.points_ref, bf16[512,512]{1,0:T(8,128)(2,1)} %pad.12.analysis_ref, bf16[512,512]{1,0:T(8,128)(2,1)} %pad.13.synthesis_ref, f32[512,1]{1,0:T(8,128)} %copy.25.decay_ref, f32[8,512]{1,0:T(8,128)} %broadcast_multiply_fusion.table_ref), custom_call_target="tpu_custom_call" | custom-call | tf_op jit(solution)/shard_map/pallas_call | solution.py:246
  370.0 0.8 slice_bitcast_fusion
  370.8 0.8 slice.33
  371.7 0.6 copy.27
  372.3 0.6 copy.31
  (30 shorter events, 0.1 us)
Async XLA Ops:
  0.6 6.4 %copy-start.13 = (bf16[64]{0:T(256)(128)(2,1)S(1)}, bf16[64]{0:T(256)(128)(2,1)}, u32[]{:S(2)}) copy-start(bf16[64]{0:T(256)(128)(2,1)} %constant.78) | copy-start | bytes 388
  1.7 6.3 %copy-start.3 = (f32[1024]{0:T(1024)S(1)}, f32[1024]{0:T(1024)}, u32[]{:S(2)}) copy-start(f32[1024]{0:T(1024)} %constant.63.clone) | copy-start | bytes 12292
  1.7 6.3 %copy-start.4 = (f32[1024]{0:T(1024)S(1)}, f32[1024]{0:T(1024)}, u32[]{:S(2)}) copy-start(f32[1024]{0:T(1024)} %constant.64.clone) | copy-start | bytes 12292
  1.7 6.3 %copy-start.5 = (f32[1024]{0:T(1024)S(1)}, f32[1024]{0:T(1024)}, u32[]{:S(2)}) copy-start(f32[1024]{0:T(1024)} %constant.68.clone) | copy-start | bytes 12292
  1.7 6.3 %copy-start.6 = (f32[1024]{0:T(1024)S(1)}, f32[1024]{0:T(1024)}, u32[]{:S(2)}) copy-start(f32[1024]{0:T(1024)} %constant.69.clone) | copy-start | bytes 12292
  1.7 6.3 %copy-start.9 = (pred[1024]{0:T(1024)(128)(4,1)S(1)}, pred[1024]{0:T(1024)(128)(4,1)}, u32[]{:S(2)}) copy-start(pred[1024]{0:T(1024)(128)(4,1)} %constant.65.clone) | copy-start | bytes 3076
  1.7 6.3 %copy-start.10 = (pred[1024]{0:T(1024)(128)(4,1)S(1)}, pred[1024]{0:T(1024)(128)(4,1)}, u32[]{:S(2)}) copy-start(pred[1024]{0:T(1024)(128)(4,1)} %constant.66.clone) | copy-start | bytes 3076
  1.7 6.3 %copy-start.11 = (pred[1024]{0:T(1024)(128)(4,1)S(1)}, pred[1024]{0:T(1024)(128)(4,1)}, u32[]{:S(2)}) copy-start(pred[1024]{0:T(1024)(128)(4,1)} %constant.67.clone) | copy-start | bytes 3076
  1.7 6.3 %copy-start.12 = (pred[1024]{0:T(1024)(128)(4,1)S(1)}, pred[1024]{0:T(1024)(128)(4,1)}, u32[]{:S(2)}) copy-start(pred[1024]{0:T(1024)(128)(4,1)} %constant.79) | copy-start | bytes 3076
  33.3 6.6 %copy-start.1 = (bf16[512,441]{0,1:T(8,128)(2,1)S(1)}, bf16[512,441]{0,1:T(8,128)(2,1)}, u32[]{:S(2)}) copy-start(bf16[512,441]{0,1:T(8,128)(2,1)} %param.23) | copy-start | bytes 1354756
  33.3 98.7 %all-to-all-start = ((bf16[16,4,32,1024]{3,2,1,0:T(8,128)(2,1)}), bf16[16,4,32,1024]{3,2,1,0:T(8,128)(2,1)}, u32[]{:S(2)}, u32[]{:S(2)}) async-start(bf16[16,4,32,1024]{3,2,1,0:T(8,128)(2,1)} %bitcast.29), calls=%async_computation | async-start | bytes 8388608 | tf_op jit(solution)/shard_map/all_to_all | solution.py:313
  39.9 1.1 copy-start
  40.0 1.9 copy-start.8
  262.1 5.5 %copy-start.2 = (f32[3,512]{1,0:T(4,128)S(1)}, f32[3,512]{1,0:T(4,128)}, u32[]{:S(2)}) copy-start(f32[3,512]{1,0:T(4,128)} %param.20) | copy-start | bytes 18436
  262.1 5.6 %copy-start.7 = (f32[512]{0:T(512)S(1)}, f32[512]{0:T(512)}, u32[]{:S(2)}) copy-start(f32[512]{0:T(512)} %param.21) | copy-start | bytes 6148
  262.1 97.7 %all-to-all-start.2 = ((bf16[32,4,32,512]{3,2,1,0:T(8,128)(2,1)}), bf16[32,4,32,512]{3,2,1,0:T(8,128)(2,1)}, u32[]{:S(2)}, u32[]{:S(2)}) async-start(bf16[32,4,32,512]{3,2,1,0:T(8,128)(2,1)} %bitcast.28), calls=%async_computation.2 | async-start | bytes 8388608 | tf_op jit(solution)/shard_map/all_to_all | solution.py:307

commit v2 on v1

--- a/solution.py
+++ b/solution.py
@@ -15,6 +15,8 @@
 transport_length = 1.5
 one_third = 1.0 / 3.0
 VMEM_LIMIT = 60 * 1024 * 1024
+MESH = pl.DeviceIdType.MESH
+CUBE = False
 
 
 def half_spectrum(ny, nz):
@@ -111,89 +113,225 @@
     return jnp.concatenate([values[..., half:], values[..., :half]], axis=-1)
 
 
-def transport_kernel(by_cell, group, nx, halves, q_ref, p_ref, c_ref, s_ref, cv_ref, sv_ref,
-                     w_ref, damping_ref, out_ref, z_ref, l_ref):
+def my_place(cube):
+    d, s, n = lax.axis_index("dir"), lax.axis_index("shard"), lax.axis_size("shard")
+    if not cube:
+        return d, s
+    half = n // 2
+    return s // half, d * half + s % half
+
+
+def place(cube, p, block):
+    if not cube:
+        return p, block
+    half = lax.axis_size("shard") // 2
+    return block // half, p * half + block % half
+
+
+def greet():
+    d, s = lax.axis_index("dir"), lax.axis_index("shard")
+    two, n = lax.axis_size("dir"), lax.axis_size("shard")
+    barrier = pltpu.get_barrier_semaphore()
+
+    def one(k, carry):
+        other = (d * n + s + k) % (two * n)
+        pl.semaphore_signal(barrier, inc=1, device_id=(other // n, other % n), device_id_type=MESH)
+        return carry
+
+    lax.fori_loop(1, two * n, one, 0)
+
+
+def greeted():
+    others = lax.axis_size("dir") * lax.axis_size("shard") - 1
+    pl.semaphore_wait(pltpu.get_barrier_semaphore(), others)
+
+
+def remote(source, target, send, receive, device):
+    return pltpu.make_async_remote_copy(
+        src_ref=source, dst_ref=target, send_sem=send, recv_sem=receive,
+        device_id=device, device_id_type=MESH,
+    )
+
+
+def is_me(device):
+    return (device[0] == lax.axis_index("dir")) & (device[1] == lax.axis_index("shard"))
+
+
+def transport_kernel(cube, by_cell, group, nx, halves, q_ref, p_ref, c_ref, s_ref, cv_ref, sv_ref,
+                     w_ref, damping_ref, out_ref, z_ref, l_ref, stage_ref, send_sem, recv_sem,
+                     local_sem):
+    greet()
     rows = nx * group
     lanes = w_ref.shape[1]
     width = lanes // halves
+    groups = p_ref.shape[0]
+    n = lax.axis_size("shard")
+    slab = nx // n
+    here = (lax.axis_index("dir"), lax.axis_index("shard"))
+    held_p, held_block = my_place(cube and by_cell)
+    new_p, _ = my_place(cube)
+    slot_me = held_p * n + held_block if halves > 1 else held_block
+
+    def target(h, t):
+        return (h, t) if halves > 1 else place(cube, held_p, t)
+
+    def origin(slot):
+        if halves > 1:
+            return place(cube, slot // n, slot % n)
+        return new_p, slot
+
+    def copy_out(g, h, t):
+        device = target(h, t)
+        return remote(
+            stage_ref.at[h, g, pl.ds(t * slab, slab)],
+            out_ref.at[slot_me, :, pl.ds(pl.multiple_of(g * group, group), group), :],
+            send_sem.at[g, h * n + t], recv_sem.at[g, slot_me], device,
+        )
+
+    def copy_here(g, h, t):
+        return pltpu.make_async_copy(
+            stage_ref.at[h, g, pl.ds(t * slab, slab)],
+            out_ref.at[slot_me, :, pl.ds(pl.multiple_of(g * group, group), group), :],
+            local_sem.at[g],
+        )
+
     col = lax.broadcasted_iota(jnp.int32, (nx, rows), 1)
     line = lax.broadcasted_iota(jnp.int32, (nx, rows), 0)
     col_x = col // group if by_cell else col % nx
     expand = jnp.where(col_x == line, 1.0, 0.0).astype(jnp.bfloat16)
-    wide = jnp.dot(p_ref[0], expand, preferred_element_type=jnp.float32)
-    row_at = lax.broadcasted_iota(jnp.int32, wide.shape, 0)
-    col_at = lax.broadcasted_iota(jnp.int32, wide.shape, 1)
-    col_m = col_at % group if by_cell else col_at // nx
-    l_ref[...] = jnp.where(row_at % group == col_m, wide, 0.0).astype(jnp.bfloat16)
-
-    outer = q_ref.shape[0]
+
     chunks = 4
+    outer = nx if by_cell else group
     part = outer // chunks
     step_rows = rows // chunks
-
-    def forward(i, carry):
-        block = to_rows(q_ref[pl.ds(i * part, part)])
-        z = jnp.dot(block, w_ref[...], preferred_element_type=jnp.float32)
-        start = pl.multiple_of(i * step_rows, step_rows)
-        z_ref[pl.ds(start, step_rows), :] = z.astype(jnp.bfloat16)
+    part_x = nx // chunks
+    per = n // chunks
+    first = held_block // per + chunks // 2
+
+    def one_group(g, carry):
+        wide = jnp.dot(p_ref[g], expand, preferred_element_type=jnp.float32)
+        row_at = lax.broadcasted_iota(jnp.int32, wide.shape, 0)
+        col_at = lax.broadcasted_iota(jnp.int32, wide.shape, 1)
+        col_m = col_at % group if by_cell else col_at // nx
+        l_ref[...] = jnp.where(row_at % group == col_m, wide, 0.0).astype(jnp.bfloat16)
+        m_at = pl.ds(pl.multiple_of(g * group, group), group)
+
+        def forward(i, carry):
+            if by_cell:
+                block = to_rows(q_ref[pl.ds(i * part, part), m_at, :])
+            else:
+                block = to_rows(q_ref[pl.ds(g * group + i * part, part)])
+            z = jnp.dot(block, w_ref[...], preferred_element_type=jnp.float32)
+            start = pl.multiple_of(i * step_rows, step_rows)
+            z_ref[pl.ds(start, step_rows), :] = z.astype(jnp.bfloat16)
+            return carry
+
+        lax.fori_loop(0, chunks, forward, 0)
+
+        ripple = jnp.dot(l_ref[rows:, :], z_ref[...], preferred_element_type=jnp.float32)
+        cross = ripple * cv_ref[m_at, :] + swap(ripple) * sv_ref[m_at, :]
+
+        @pl.when(g == 0)
+        def _():
+            greeted()
+
+        def backward(j, carry):
+            i = (first + j) % chunks
+            start = pl.multiple_of(i * step_rows, step_rows)
+            y = jnp.dot(l_ref[pl.ds(start, step_rows), :], z_ref[...],
+                        preferred_element_type=jnp.float32)
+            y = y.reshape(part_x, group, lanes)
+            odd = lax.broadcasted_iota(jnp.int32, y.shape, 0) % 2 == 1
+            turned = y * c_ref[m_at, :][None] + swap(y) * s_ref[m_at, :][None]
+            turned = turned + jnp.where(odd, -cross[None], cross[None])
+            turned = turned.reshape(step_rows, lanes).astype(jnp.bfloat16)
+            back = lax.dot_general(turned, w_ref[...], (((1,), (1,)), ((), ())),
+                                   preferred_element_type=jnp.float32)
+            x_at = pl.ds(pl.multiple_of(i * part_x, part_x), part_x)
+            back = back.reshape(part_x, group, lanes) * damping_ref[x_at, :][:, None, :]
+            back = back.astype(jnp.bfloat16)
+            for h in range(halves):
+                stage_ref[h, g, x_at] = back[:, :, h * width : (h + 1) * width]
+
+            def send(k, carry):
+                t = i * per + (held_block + k) % per
+                for h in range(halves):
+                    mine = is_me(target(h, t))
+
+                    @pl.when(mine)
+                    def _():
+                        copy_here(g, h, t).start()
+
+                    @pl.when(jnp.logical_not(mine))
+                    def _():
+                        copy_out(g, h, t).start()
+                return carry
+
+            lax.fori_loop(0, per, send, 0)
+            return carry
+
+        lax.fori_loop(0, chunks, backward, 0)
         return carry
 
-    lax.fori_loop(0, chunks, forward, 0)
-
-    ripple = jnp.dot(l_ref[rows:, :], z_ref[...], preferred_element_type=jnp.float32)
-    cross = ripple * cv_ref[...] + swap(ripple) * sv_ref[...]
-    part_x = nx // chunks
-
-    def backward(i, carry):
-        start = pl.multiple_of(i * step_rows, step_rows)
-        y = jnp.dot(l_ref[pl.ds(start, step_rows), :], z_ref[...],
-                    preferred_element_type=jnp.float32)
-        y = y.reshape(part_x, group, lanes)
-        odd = lax.broadcasted_iota(jnp.int32, y.shape, 0) % 2 == 1
-        turned = y * c_ref[...][None] + swap(y) * s_ref[...][None]
-        turned = turned + jnp.where(odd, -cross[None], cross[None])
-        turned = turned.reshape(step_rows, lanes).astype(jnp.bfloat16)
-        back = lax.dot_general(turned, w_ref[...], (((1,), (1,)), ((), ())),
-                               preferred_element_type=jnp.float32)
-        x_at = pl.multiple_of(i * part_x, part_x)
-        back = back.reshape(part_x, group, lanes) * damping_ref[pl.ds(x_at, part_x), :][:, None, :]
-        back = back.astype(jnp.bfloat16)
-        for h in range(halves):
-            out_ref[h, pl.ds(x_at, part_x)] = back[:, :, h * width : (h + 1) * width]
+    lax.fori_loop(0, groups, one_group, 0)
+
+    def finish(g, carry):
+        def sent(t, carry):
+            for h in range(halves):
+                mine = is_me(target(h, t))
+
+                @pl.when(mine)
+                def _():
+                    copy_here(g, h, t).wait()
+
+                @pl.when(jnp.logical_not(mine))
+                def _():
+                    copy_out(g, h, t).wait_send()
+            return carry
+
+        lax.fori_loop(0, n, sent, 0)
+
+        def received(slot, carry):
+            @pl.when(jnp.logical_not(is_me(origin(slot))))
+            def _():
+                remote(
+                    stage_ref.at[0, g, pl.ds(0, slab)],
+                    out_ref.at[slot, :, pl.ds(pl.multiple_of(g * group, group), group), :],
+                    send_sem.at[g, slot], recv_sem.at[g, slot], here,
+                ).wait_recv()
+            return carry
+
+        lax.fori_loop(0, halves * n, received, 0)
         return carry
 
-    lax.fori_loop(0, chunks, backward, 0)
-
-
-def transport(q, by_cell, halves, operator, tables, basis, damping):
+    lax.fori_loop(0, groups, finish, 0)
+
+
+def transport(cube, q, by_cell, halves, operator, tables, basis, damping):
     nx, lanes = damping.shape
     count = q.shape[1] if by_cell else q.shape[0]
     group = operator.shape[1] // (nx + 1)
     rows = nx * group
-
-
-    if by_cell:
-        q_spec = pl.BlockSpec((nx, group, lanes), lambda g: (0, g, 0))
-    else:
-        q_spec = pl.BlockSpec((group, nx, lanes), lambda g: (g, 0, 0))
-    table_spec = pl.BlockSpec((group, lanes), lambda g: (g, 0))
+    groups = count // group
+    n = lax.axis_size("shard")
+    width = lanes // halves
+    vmem = pl.BlockSpec(memory_space=pltpu.VMEM)
     return pl.pallas_call(
-        functools.partial(transport_kernel, by_cell, group, nx, halves),
-        out_shape=jax.ShapeDtypeStruct((halves, nx, count, lanes // halves), jnp.bfloat16),
-        grid=(count // group,),
-        in_specs=[
-            q_spec,
-            pl.BlockSpec((1, rows + group, nx), lambda g: (g, 0, 0)),
-            table_spec, table_spec, table_spec, table_spec,
-            pl.BlockSpec((lanes, lanes), lambda g: (0, 0)),
-            pl.BlockSpec((nx, lanes), lambda g: (0, 0)),
-        ],
-        out_specs=pl.BlockSpec((halves, nx, group, lanes // halves), lambda g: (0, 0, g, 0)),
+        functools.partial(transport_kernel, cube, by_cell, group, nx, halves),
+        out_shape=jax.ShapeDtypeStruct((halves * n, nx // n, count, width), jnp.bfloat16),
+        in_specs=[vmem] * 8,
+        out_specs=pl.BlockSpec(memory_space=pl.ANY),
         scratch_shapes=[
             pltpu.VMEM((rows, lanes), jnp.bfloat16),
             pltpu.VMEM((rows + group, rows), jnp.bfloat16),
+            pltpu.VMEM((halves, groups, nx, group, width), jnp.bfloat16),
+            pltpu.SemaphoreType.DMA((groups, halves * n)),
+            pltpu.SemaphoreType.DMA((groups, halves * n)),
+            pltpu.SemaphoreType.DMA((groups,)),
         ],
-        compiler_params=pltpu.CompilerParams(vmem_limit_bytes=VMEM_LIMIT),
+        compiler_params=pltpu.CompilerParams(
+            vmem_limit_bytes=VMEM_LIMIT, collective_id=2 if by_cell else 0, has_side_effects=True
+        ),
     )(q, operator, *tables, basis, damping)
 
 
@@ -203,30 +341,76 @@
     return jnp.dot(synthesis_ref[...], harmonic, preferred_element_type=jnp.float32)
 
 
-def diffuse_kernel(points_ref, analysis_ref, synthesis_ref, decay_ref, out_ref):
-    n, _, count, width = points_ref.shape
-    block = to_rows(points_ref[:, 0])
-    mixed = mix(block, analysis_ref, synthesis_ref, decay_ref)
-    out_ref[:, 0] = mixed.reshape(n, count, width).astype(jnp.bfloat16)
-
-
-def diffuse(points, analysis, synthesis, decay):
-    n, rows, count, lanes = points.shape
+def diffuse_kernel(cube, points_ref, analysis_ref, synthesis_ref, decay_ref, out_ref, stage_ref,
+                   send_sem, recv_sem, local_sem):
+    greet()
+    n, slab, count, lanes = points_ref.shape
+    here = (lax.axis_index("dir"), lax.axis_index("shard"))
+    p, me = my_place(cube)
     width = lanes // 2
-    spec = pl.BlockSpec((n, 1, count, width), lambda i, j: (0, i, 0, j))
-    whole = pl.BlockSpec(analysis.shape, lambda i, j: (0, 0))
+
+    def copy_out(i, t):
+        return remote(stage_ref.at[t, i], out_ref.at[me * slab + i], send_sem.at[i, t],
+                      recv_sem.at[i, me], place(cube, p, t))
+
+    def copy_here(i):
+        return pltpu.make_async_copy(stage_ref.at[me, i], out_ref.at[me * slab + i],
+                                     local_sem.at[i])
+
+    def one_row(i, carry):
+        for j in range(2):
+            at = slice(j * width, (j + 1) * width)
+            block = to_rows(points_ref[:, i, :, at])
+            mixed = mix(block, analysis_ref, synthesis_ref, decay_ref)
+            stage_ref[:, i, :, at] = mixed.reshape(n, count, width).astype(jnp.bfloat16)
+
+        @pl.when(i == 0)
+        def _():
+            greeted()
+
+        def send(k, carry):
+            copy_out(i, (me + n // 2 + k) % n).start()
+            return carry
+
+        lax.fori_loop(0, n // 2, send, 0)
+        lax.fori_loop(n // 2 + 1, n, send, 0)
+        copy_here(i).start()
+        return carry
+
+    lax.fori_loop(0, slab, one_row, 0)
+
+    def finish(i, carry):
+        def one(k, carry):
+            t = (me + k) % n
+            copy_out(i, t).wait_send()
+            remote(stage_ref.at[t, i], out_ref.at[t * slab + i], send_sem.at[i, t],
+                   recv_sem.at[i, t], here).wait_recv()
+            return carry
+
+        lax.fori_loop(1, n, one, 0)
+        copy_here(i).wait()
+        return carry
+
+    lax.fori_loop(0, slab, finish, 0)
+
+
+def diffuse(cube, points, analysis, synthesis, decay):
+    n, slab, count, lanes = points.shape
+    vmem = pl.BlockSpec(memory_space=pltpu.VMEM)
     return pl.pallas_call(
-        diffuse_kernel,
-        out_shape=jax.ShapeDtypeStruct(points.shape, jnp.bfloat16),
-        grid=(rows, 2),
-        in_specs=[
-            spec,
-            whole,
-            pl.BlockSpec(synthesis.shape, lambda i, j: (0, 0)),
-            pl.BlockSpec(decay.shape, lambda i, j: (0, 0)),
+        functools.partial(diffuse_kernel, cube),
+        out_shape=jax.ShapeDtypeStruct((n * slab, count, lanes), jnp.bfloat16),
+        in_specs=[vmem] * 4,
+        out_specs=pl.BlockSpec(memory_space=pl.ANY),
+        scratch_shapes=[
+            pltpu.VMEM(points.shape, jnp.bfloat16),
+            pltpu.SemaphoreType.DMA((slab, n)),
+            pltpu.SemaphoreType.DMA((slab, n)),
+            pltpu.SemaphoreType.DMA((slab,)),
         ],
-        out_specs=spec,
-        compiler_params=pltpu.CompilerParams(vmem_limit_bytes=VMEM_LIMIT),
+        compiler_params=pltpu.CompilerParams(
+            vmem_limit_bytes=VMEM_LIMIT, collective_id=1, has_side_effects=True
+        ),
     )(points, analysis, synthesis, decay)
 
 
@@ -280,15 +464,7 @@
     state = propagators[0]
     count, nx, lanes = state.shape
     nz = lanes // NY
-    shards = lax.axis_size("shard")
     group = min(16, count)
-    offset = lax.axis_index("shard") * count
-    heading = lax.dynamic_slice_in_dim(orient, offset, count, 1)
-    direction = 1.0 - 2.0 * lax.axis_index("dir").astype(jnp.float32)
-    scale = direction * transport_length
-    operator, nyquist = line_operator(heading, scale, nx, group)
-    cu, su, cv, sv = plane_tables(heading, scale, NY, nz)
-    tables = (cu, su, cv * nyquist, sv * nyquist)
     basis = jnp.asarray(real_basis(NY, nz).astype(jnp.bfloat16))
     damping = jnp.exp(-field)
     harmonics, total = analysis.shape
@@ -297,24 +473,27 @@
     synthesis = jnp.pad(synthesis, ((0, 0), (0, pad)))
     decay = jnp.pad(decay, (0, pad))[:, None]
 
-    by_cell = False
+    def held(p, block):
+        heading = lax.dynamic_slice_in_dim(orient, block * count, count, 1)
+        scale = (1.0 - 2.0 * p.astype(jnp.float32)) * transport_length
+        operator, nyquist = line_operator(heading, scale, nx, group)
+        cu, su, cv, sv = plane_tables(heading, scale, NY, nz)
+        return operator, (cu, su, cv * nyquist, sv * nyquist)
+
+    staged = held(*my_place(False))
     for contour in range(STEPS):
+        by_cell = contour > 0
+        if contour == 1 and CUBE:
+            staged = held(*my_place(True))
         is_last = contour == STEPS - 1
         halves = lax.axis_size("dir") if is_last else 1
-        moved = transport(state, by_cell, halves, operator, tables, basis, damping)
+        moved = transport(CUBE, state, by_cell, halves, *staged, basis, damping)
         if is_last:
-            moved = moved.reshape(halves * shards, nx // shards, count, lanes // halves)
-            moved = lax.all_to_all(moved, ("dir", "shard"), 0, 0, tiled=True)
-            moved = moved.reshape(halves, shards, nx // shards, count, lanes // halves)
+            moved = moved.reshape((halves, moved.shape[0] // halves) + moved.shape[1:])
             table = moment_table(orient, quad_weights)
             result = moments(moved, analysis, synthesis, decay, table)
         else:
-            moved = moved.reshape(shards, nx // shards, count, lanes)
-            moved = lax.all_to_all(moved, "shard", 0, 0, tiled=True)
-            mixed = diffuse(moved, analysis, synthesis, decay)
-            mixed = lax.all_to_all(mixed, "shard", 0, 0, tiled=True)
-            state = mixed.reshape(nx, count, lanes)
-            by_cell = True
+            state = diffuse(CUBE, moved, analysis, synthesis, decay)
     return result[:, 0], jnp.moveaxis(result[:, 1:6], 1, 0)
 
 

time: 377 us -> 330 us (0.88); the launches traced: 373 us -> 330 us
  Pallas kernels: 66.5 us -> 314 us
  waiting for transfers between devices: 181 us -> 0 us
  blocking collectives: 97 us -> 0 us
  starting transfers between devices: 12.1 us -> 0 us
    pallas_call x3, Pallas kernels: 56.4 us -> 304 us  [the longest x2 208 us: transport(): pl.pallas_call(functools.partial(transport_kernel, cube, by_cell, group,...]
    all_to_all x2 -> x0, waiting for transfers between devices: 181 us -> none  [the longest x1 91.6 us: on_device(): moved = lax.all_to_all(moved, ('dir', 'shard'), 0, 0, tiled=True)]
    all_to_all x1 -> x0, blocking collectives: 97 us -> none  [on_device(): mixed = lax.all_to_all(mixed, 'shard', 0, 0, tiled=True)]
    all_to_all x2 -> x0, starting transfers between devices: 12.1 us -> none  [the longest x1 6.6 us: on_device(): moved = lax.all_to_all(moved, 'shard', 0, 0, tiled=True)]
  transfers between devices with their start and end apart: 2 -> 0, of which waited for: 2 -> 0; matrix products, arithmetic and copies ran while one was open for 1% -> 0% of each run, Pallas kernels for 0% -> 0%
where the time goes in v2:
time: 330 us
  Pallas kernels  314 us (95%)
  local copies, waits for them, and re-layouts  6.74 us (2%)
  other arithmetic  5.98 us (2%)
    pallas_call x2, Pallas kernels, transport(): pl.pallas_call(functools.partial(transport_kernel, cube, by_cell, group,...  208 us
    pallas_call x1, Pallas kernels, diffuse(): pl.pallas_call(functools.partial(diffuse_kernel, cube), out_shape=jax.Sha...  95.9 us
    pallas_call x1, Pallas kernels, moments(): pl.pallas_call(moment_kernel, out_shape=jax.ShapeDtypeStruct((rows, table...  10.1 us

profile of v2, /device:TPU:19, one launch (start us, length us, event | category | flops | bytes accessed | tf_op | source)
XLA Modules:
  0.0 330.0 jit_solution(2217870303426001194)
XLA Ops:
  0.6 0.0 copy-start.6
  0.6 0.8 constant_dynamic-slice_fusion
  1.4 0.1 multiply_bitcast_fusion
  1.5 0.0 copy-start.2
  1.5 2.8 fusion.23
  4.3 0.1 mul.237
  4.4 0.8 multiply_cosine_fusion.2
  5.2 0.1 cos.30
  5.3 2.7 convolution_convert_fusion
  8.0 0.0 copy-done.6
  8.0 0.9 pad_maximum_fusion.p_ref
  9.0 0.0 copy-done.2
  9.0 0.7 negate_exponential_fusion.damping_ref
  9.7 101.7 %shard_map.185.points_ref = bf16[16,4,32,1024]{3,2,1,0:T(8,128)(2,1)} custom-call(bf16[32,64,1024]{2,1,0:T(8,128)(2,1)} %bitcast.26, bf16[2,1040,64]{2,1,0:T(8,128)(2,1)} %pad_maximum_fusion.p_ref, f32[32,1024]{1,0:T(8,128)} %get-tuple-element.11.c_ref, f32[32,1024]{1,0:T(8,128)} %get-tuple-element.9.s_ref, f32[32,1024]{1,0:T(8,128)} %get-tuple-element.10.cv_ref, ...), custom_call_target="tpu_custom_call" | custom-call | tf_op jit(solution)/shard_map/pallas_call | solution.py:319
  111.4 0.0 copy-done.1
  111.4 0.0 copy-start
  111.4 0.0 copy-start.5
  111.4 0.2 copy.24
  111.6 0.9 pad.13.synthesis_ref
  112.5 0.9 pad.12.analysis_ref
  113.4 0.9 copy.25.decay_ref
  114.2 95.9 %shard_map.186.q_ref = bf16[64,32,1024]{2,1,0:T(8,128)(2,1)} custom-call(bf16[16,4,32,1024]{3,2,1,0:T(8,128)(2,1)} %shard_map.185.points_ref, bf16[512,512]{1,0:T(8,128)(2,1)} %pad.12.analysis_ref, bf16[512,512]{1,0:T(8,128)(2,1)} %pad.13.synthesis_ref, f32[512,1]{1,0:T(8,128)} %copy.25.decay_ref), custom_call_target="tpu_custom_call" | custom-call | tf_op jit(solution)/shard_map/pallas_call | solution.py:400
  210.1 0.0 copy-start.3
  210.1 0.0 copy-start.4
  210.1 106.1 %shard_map.187 = bf16[32,4,32,512]{3,2,1,0:T(8,128)(2,1)} custom-call(bf16[64,32,1024]{2,1,0:T(8,128)(2,1)} %shard_map.186.q_ref, bf16[2,1040,64]{2,1,0:T(8,128)(2,1)} %pad_maximum_fusion.p_ref, f32[32,1024]{1,0:T(8,128)} %get-tuple-element.11.c_ref, f32[32,1024]{1,0:T(8,128)} %get-tuple-element.9.s_ref, f32[32,1024]{1,0:T(8,128)} %get-tuple-element.10.cv_ref, ...), custom_call_target="tpu_custom_call" | custom-call | tf_op jit(solution)/shard_map/pallas_call | solution.py:319
  316.3 0.0 copy-done.4
  316.3 0.6 broadcast_multiply_fusion.table_ref
  316.9 10.1 %shard_map.188 = f32[4,8,512]{2,1,0:T(8,128)} custom-call(bf16[2,16,4,32,512]{4,3,2,1,0:T(8,128)(2,1)} %bitcast.25, bf16[512,512]{1,0:T(8,128)(2,1)} %pad.12.analysis_ref, bf16[512,512]{1,0:T(8,128)(2,1)} %pad.13.synthesis_ref, f32[512,1]{1,0:T(8,128)} %copy.25.decay_ref, f32[8,512]{1,0:T(8,128)} %broadcast_multiply_fusion.table_ref), custom_call_target="tpu_custom_call" | custom-call | tf_op jit(solution)/shard_map/pallas_call | solution.py:430
  327.0 0.8 slice_bitcast_fusion
  327.9 0.6 copy.27
  328.5 0.8 slice.33
  329.4 0.6 copy.31
  (11 shorter events, 0.1 us)
Async XLA Ops:
  0.6 7.4 %copy-start.6 = (bf16[64]{0:T(256)(128)(2,1)S(1)}, bf16[64]{0:T(256)(128)(2,1)}, u32[]{:S(2)}) copy-start(bf16[64]{0:T(256)(128)(2,1)} %constant.78) | copy-start | bytes 388
  1.5 7.5 %copy-start.2 = (f32[64,1024]{1,0:T(8,128)S(1)}, f32[64,1024]{1,0:T(8,128)}, u32[]{:S(2)}) copy-start(f32[64,1024]{1,0:T(8,128)} %param.19) | copy-start | bytes 786436
  9.7 101.7 %copy-start.1 = (bf16[512,441]{0,1:T(8,128)(2,1)S(1)}, bf16[512,441]{0,1:T(8,128)(2,1)}, u32[]{:S(2)}) copy-start(bf16[512,441]{0,1:T(8,128)(2,1)} %param.23) | copy-start | bytes 1354756
  111.4 1.1 copy-start
  111.4 2.0 copy-start.5
  210.1 106.1 %copy-start.3 = (f32[3,512]{1,0:T(4,128)S(1)}, f32[3,512]{1,0:T(4,128)}, u32[]{:S(2)}) copy-start(f32[3,512]{1,0:T(4,128)} %param.20) | copy-start | bytes 18436
  210.1 106.2 %copy-start.4 = (f32[512]{0:T(512)S(1)}, f32[512]{0:T(512)}, u32[]{:S(2)}) copy-start(f32[512]{0:T(512)} %param.21) | copy-start | bytes 6148

commit v3 on v1

v3 whole, which is shorter than its diff:
```python
import functools
import math

import jax
import jax.numpy as jnp
import numpy as np
from jax import lax
from jax.experimental import pallas as pl
from jax.experimental.pallas import tpu as pltpu
from jax.sharding import PartitionSpec as P

NY = 64

transport_length = 1.5
one_third = 1.0 / 3.0
VMEM_LIMIT = 60 * 1024 * 1024
MESH = pl.DeviceIdType.MESH


def half_spectrum(ny, nz):
    selfs = [(0, 0), (ny // 2, 0), (0, nz // 2), (ny // 2, nz // 2)]
    pairs = []
    for ky in range(ny):
        for kz in range(nz):
            mirror = ((-ky) % ny, (-kz) % nz)
            if (ky, kz) < mirror:
                pairs.append((ky, kz))
    first = selfs[:2] + pairs
    second = selfs[2:] + pairs
    return np.array(first + second, np.int64)


def real_basis(ny, nz):
    freq = half_spectrum(ny, nz)
    half = len(freq) // 2
    y = np.repeat(np.arange(ny), nz)[:, None]
    z = np.tile(np.arange(nz), ny)[:, None]
    angle = 2.0 * np.pi * (y * freq[None, :, 0] / ny + z * freq[None, :, 1] / nz)
    basis = np.cos(angle)
    basis[:, half + 2 :] = -np.sin(angle[:, half + 2 :])
    return basis


def signed(k, length):
    return np.where(k <= (length - 1) // 2, k, k - length) * (2.0 * np.pi / length)


def plane_tables(heading, scale, ny, nz):
    freq = half_spectrum(ny, nz)
    lanes = len(freq)
    half = lanes // 2
    wave_y = jnp.asarray(signed(freq[:, 0], ny), jnp.float32)
    wave_z = jnp.asarray(signed(freq[:, 1], nz), jnp.float32)
    theta_y = scale * heading[1][:, None] * wave_y[None, :]
    theta_z = scale * heading[2][:, None] * wave_z[None, :]
    cy, sy, cz, sz = jnp.cos(theta_y), jnp.sin(theta_y), jnp.cos(theta_z), jnp.sin(theta_z)
    ny_mask = freq[:, 0] == ny // 2
    nz_mask = freq[:, 1] == nz // 2
    only_y = jnp.asarray(ny_mask & ~nz_mask)[None]
    only_z = jnp.asarray(nz_mask & ~ny_mask)[None]
    both = jnp.asarray(ny_mask & nz_mask)[None]
    cos_sum = cy * cz - sy * sz
    sin_sum = sy * cz + cy * sz
    single = only_y | only_z
    cu = jnp.where(single, cy * cz, cos_sum)
    su = jnp.where(only_z, sy * cz, jnp.where(only_y, sz * cy, jnp.where(both, 0.0, sin_sum)))
    cv = jnp.where(
        only_z, -cy * sz, jnp.where(only_y, -cz * sy, jnp.where(both, -sin_sum, 0.0))
    )
    sv = jnp.where(single, -sy * sz, 0.0)
    weight = np.full((lanes,), 2.0 / (ny * nz))
    weight[[0, 1, half, half + 1]] = 1.0 / (ny * nz)
    turn = np.where(np.arange(lanes) < half, 1.0, -1.0)
    weight = jnp.asarray(weight, jnp.float32)[None]
    turn = jnp.asarray(turn, jnp.float32)[None]
    return cu * weight, su * weight * turn, cv * weight, sv * weight * turn


def line_operator(heading, scale, nx, group):
    count = heading.shape[1]
    k = np.arange(1, nx // 2)
    theta = scale * heading[0][:, None] * jnp.asarray(k * (2.0 * np.pi / nx), jnp.float32)[None]
    theta_n = -scale * heading[0][:, None] * math.pi
    trig = jnp.concatenate(
        [jnp.ones((count, 1), jnp.float32), jnp.cos(theta), jnp.sin(theta), jnp.cos(theta_n)], 1
    )
    gap = (np.arange(nx)[:, None] - np.arange(nx)[None, :]) % nx
    angle = 2.0 * np.pi * ((k[:, None, None] * gap[None]) % nx) / nx
    rows = np.concatenate(
        [np.ones((1, nx, nx)), 2 * np.cos(angle), 2 * np.sin(angle), (1.0 - 2.0 * (gap % 2))[None]]
    )
    table = jnp.asarray(rows / nx, jnp.float32)
    operator = jnp.einsum("gmk,kax->gamx", trig.reshape(-1, group, nx), table,
                          precision=lax.Precision.HIGHEST)
    operator = operator.reshape(count // group, nx * group, nx)
    sign = jnp.asarray(1.0 - 2.0 * (np.arange(nx) % 2), jnp.float32)
    extra = jnp.broadcast_to(sign, (count // group, group, nx))
    operator = jnp.concatenate([operator, extra], 1).astype(jnp.bfloat16)
    return operator, jnp.sin(theta_n) / nx


def to_rows(block):
    a, b, lanes = block.shape
    if b % 16:
        return block.astype(jnp.float32).reshape(a * b, lanes).astype(jnp.bfloat16)
    return block.reshape(a * b, lanes)


def swap(values):
    half = values.shape[-1] // 2
    return jnp.concatenate([values[..., half:], values[..., :half]], axis=-1)


def greet():
    d, s = lax.axis_index("dir"), lax.axis_index("shard")
    two, n = lax.axis_size("dir"), lax.axis_size("shard")
    barrier = pltpu.get_barrier_semaphore()

    def one(k, carry):
        other = (d * n + s + k) % (two * n)
        pl.semaphore_signal(barrier, inc=1, device_id=(other // n, other % n), device_id_type=MESH)
        return carry

    lax.fori_loop(1, two * n, one, 0)


def greeted():
    others = lax.axis_size("dir") * lax.axis_size("shard") - 1
    pl.semaphore_wait(pltpu.get_barrier_semaphore(), others)


def remote(source, target, send, receive, device):
    return pltpu.make_async_remote_copy(
        src_ref=source, dst_ref=target, send_sem=send, recv_sem=receive,
        device_id=device, device_id_type=MESH,
    )


def is_me(device):
    return (device[0] == lax.axis_index("dir")) & (device[1] == lax.axis_index("shard"))


def transport(by_cell, halves, group, nx, q_ref, p_ref, tables, w_ref, damping_ref, z_ref, l_ref,
              stage_ref, ready, send):
    c_ref, s_ref, cv_ref, sv_ref = tables
    rows = nx * group
    lanes = w_ref.shape[1]
    width = lanes // halves
    groups = p_ref.shape[0]
    col = lax.broadcasted_iota(jnp.int32, (nx, rows), 1)
    line = lax.broadcasted_iota(jnp.int32, (nx, rows), 0)
    col_x = col // group if by_cell else col % nx
    expand = jnp.where(col_x == line, 1.0, 0.0).astype(jnp.bfloat16)

    chunks = 4
    part = (nx if by_cell else group) // chunks
    step_rows = rows // chunks
    part_x = nx // chunks
    first = lax.axis_index("shard") // (lax.axis_size("shard") // chunks) + chunks // 2

    def one_group(g, carry):
        wide = jnp.dot(p_ref[g], expand, preferred_element_type=jnp.float32)
        row_at = lax.broadcasted_iota(jnp.int32, wide.shape, 0)
        col_at = lax.broadcasted_iota(jnp.int32, wide.shape, 1)
        col_m = col_at % group if by_cell else col_at // nx
        l_ref[...] = jnp.where(row_at % group == col_m, wide, 0.0).astype(jnp.bfloat16)
        m_at = pl.ds(pl.multiple_of(g * group, group), group)
        if by_cell:
            ready(g)

        def forward(i, carry):
            if by_cell:
                block = to_rows(q_ref[g, pl.ds(i * part, part)])
            else:
                block = to_rows(q_ref[pl.ds(g * group + i * part, part)])
            z = jnp.dot(block, w_ref[...], preferred_element_type=jnp.float32)
            start = pl.multiple_of(i * step_rows, step_rows)
            z_ref[pl.ds(start, step_rows), :] = z.astype(jnp.bfloat16)
            return carry

        lax.fori_loop(0, chunks, forward, 0)

        ripple = jnp.dot(l_ref[rows:, :], z_ref[...], preferred_element_type=jnp.float32)
        cross = ripple * cv_ref[m_at, :] + swap(ripple) * sv_ref[m_at, :]
        if not by_cell:

            @pl.when(g == 0)
            def _():
                ready(g)

        def backward(j, carry):
            i = (first + j) % chunks
            start = pl.multiple_of(i * step_rows, step_rows)
            y = jnp.dot(l_ref[pl.ds(start, step_rows), :], z_ref[...],
                        preferred_element_type=jnp.float32)
            y = y.reshape(part_x, group, lanes)
            odd = lax.broadcasted_iota(jnp.int32, y.shape, 0) % 2 == 1
            turned = y * c_ref[m_at, :][None] + swap(y) * s_ref[m_at, :][None]
            turned = turned + jnp.where(odd, -cross[None], cross[None])
            turned = turned.reshape(step_rows, lanes).astype(jnp.bfloat16)
            back = lax.dot_general(turned, w_ref[...], (((1,), (1,)), ((), ())),
                                   preferred_element_type=jnp.float32)
            x_at = pl.ds(pl.multiple_of(i * part_x, part_x), part_x)
            back = back.reshape(part_x, group, lanes) * damping_ref[x_at, :][:, None, :]
            back = back.astype(jnp.bfloat16)
            for h in range(halves):
                stage_ref[h, g, x_at] = back[:, :, h * width : (h + 1) * width]
            send(g, i)
            return carry

        lax.fori_loop(0, chunks, backward, 0)
        return carry

    lax.fori_loop(0, groups, one_group, 0)


def loop(low, high, body):
    def step(k, carry):
        body(k)
        return carry

    lax.fori_loop(low, high, step, 0)


def chain_kernel(group, nx, q_ref, p_ref, c_ref, s_ref, cv_ref, sv_ref, w_ref, damping_ref,
                 analysis_ref, synthesis_ref, decay_ref, table_ref, out_ref, z_ref, l_ref,
                 stage1, stage2, stage3, recv1, recv2, recv3,
                 ssem1, rsem1, lsem1, ssem2, rsem2, lsem2, ssem3, rsem3, lsem3):
    greet()
    d, me = lax.axis_index("dir"), lax.axis_index("shard")
    two, n = lax.axis_size("dir"), lax.axis_size("shard")
    here = (d, me)
    groups = p_ref.shape[0]
    slab = nx // n
    parts = min(2, slab)
    some = slab // parts
    lanes = w_ref.shape[1]
    width = lanes // two
    chunks = 4
    per = n // chunks
    tables = (c_ref, s_ref, cv_ref, sv_ref)

    def to1(g, a, t):
        return stage1.at[0, g, pl.ds(t * slab + a * some, some)]

    def at1(g, a, source):
        return recv1.at[a, g, source]

    def out1(g, a, t):
        return remote(to1(g, a, t), at1(g, a, me), ssem1.at[g, a, t], rsem1.at[g, a, me], (d, t))

    def own1(g, a):
        return pltpu.make_async_copy(to1(g, a, me), at1(g, a, me), lsem1.at[g, a])

    def issue1(g, i, a):
        def one(k):
            t = i * per + (me + k) % per

            @pl.when(t == me)
            def _():
                own1(g, a).start()

            @pl.when(t != me)
            def _():
                out1(g, a, t).start()

        loop(0, per, one)

    def out2(g, i, t):
        return remote(stage2.at[g, i, t], recv2.at[g, me * slab + i], ssem2.at[g, i, t],
                      rsem2.at[g, i, me], (d, t))

    def own2(g, i):
        return pltpu.make_async_copy(stage2.at[g, i, me], recv2.at[g, me * slab + i],
                                     lsem2.at[g, i])

    def to3(g, a, h, t):
        return stage3.at[h, g, pl.ds(t * slab + a * some, some)]

    def at3(g, a, p, source):
        return recv3.at[a, p, g, source]

    def out3(g, a, h, t):
        return remote(to3(g, a, h, t), at3(g, a, d, me), ssem3.at[g, a, h * n + t],
                      rsem3.at[g, a, d * n + me], (h, t))

    def own3(g, a):
        return pltpu.make_async_copy(to3(g, a, d, me), at3(g, a, d, me), lsem3.at[g, a])

    def issue3(g, i, a):
        def one(k):
            t = i * per + (me + k) % per
            for h in range(two):
                mine = (t == me) & (d == h)

                @pl.when(mine)
                def _():
                    own3(g, a).start()

                @pl.when(jnp.logical_not(mine))
                def _():
                    out3(g, a, h, t).start()

        loop(0, per, one)

    first = me // per + chunks // 2

    def late(issue):
        for a in range(1, parts):
            loop(0, groups, lambda g: loop(0, chunks, lambda j: issue(g, (first + j) % chunks, a)))

    transport(False, 1, group, nx, q_ref, p_ref, tables, w_ref, damping_ref, z_ref, l_ref, stage1,
              lambda g: greeted(), lambda g, i: issue1(g, i, 0))
    late(issue1)

    for a in range(parts):
        def arrived1(g):
            def one(k):
                source = (me + k) % n
                remote(to1(g, a, me), at1(g, a, source), ssem1.at[g, a, me],
                       rsem1.at[g, a, source], here).wait_recv()

            loop(1, n, one)
            own1(g, a).wait()

        loop(0, groups, arrived1)

        def row1(r):
            i = a * some + r
            for j in range(2):
                at = slice(j * (lanes // 2), (j + 1) * (lanes // 2))
                block = jnp.concatenate(
                    [to_rows(recv1[a, g, :, r, :, at]) for g in range(groups)], axis=0
                )
                mixed = mix(block, analysis_ref, synthesis_ref, decay_ref)
                mixed = mixed.reshape(groups, n, group, lanes // 2).astype(jnp.bfloat16)
                for g in range(groups):
                    stage2[g, i, :, :, at] = mixed[g]

        loop(0, some, row1)

        def send2(g):
            def row(r):
                i = a * some + r
                loop(0, n // 2, lambda k: out2(g, i, (me + n // 2 + k) % n).start())
                loop(n // 2 + 1, n, lambda k: out2(g, i, (me + n // 2 + k) % n).start())
                own2(g, i).start()

            loop(0, some, row)

        loop(0, groups, send2)

    def arrived2(g):
        def row(i):
            def one(k):
                source = (me + k) % n
                remote(stage2.at[g, i, me], recv2.at[g, source * slab + i], ssem2.at[g, i, me],
                       rsem2.at[g, i, source], here).wait_recv()

            loop(1, n, one)
            own2(g, i).wait()

        loop(0, slab, row)

    transport(True, two, group, nx, recv2, p_ref, tables, w_ref, damping_ref, z_ref, l_ref, stage3,
              arrived2, lambda g, i: issue3(g, i, 0))
    late(issue3)

    for a in range(parts):
        def arrived3(g):
            def one(k):
                slot = (d * n + me + k) % (two * n)
                remote(to3(g, a, 0, me), at3(g, a, slot // n, slot % n), ssem3.at[g, a, 0],
                       rsem3.at[g, a, slot], here).wait_recv()

            loop(1, two * n, one)
            own3(g, a).wait()

        loop(0, groups, arrived3)

        def row3(r):
            product = None
            for p in range(two):
                block = jnp.concatenate(
                    [to_rows(recv3[a, p, g, :, r]) for g in range(groups)], axis=0
                )
                mixed = mix(block, analysis_ref, synthesis_ref, decay_ref)
                mixed = mixed.astype(jnp.bfloat16).astype(jnp.float32)
                product = mixed if product is None else product * mixed
            out_ref[a * some + r] = jnp.dot(table_ref[...], product,
                                            precision=lax.Precision.HIGHEST,
                                            preferred_element_type=jnp.float32)

        loop(0, some, row3)

    def sent(g):
        for a in range(parts):
            loop(1, n, lambda k: out1(g, a, (me + k) % n).wait_send())

            def one3(k):
                slot = (d * n + me + k) % (two * n)
                out3(g, a, slot // n, slot % n).wait_send()

            loop(1, two * n, one3)
        loop(0, slab, lambda i: loop(1, n, lambda k: out2(g, i, (me + k) % n).wait_send()))

    loop(0, groups, sent)


def chain(q, operator, tables, basis, damping, analysis, synthesis, decay, table):
    nx, lanes = damping.shape
    count = q.shape[0]
    group = operator.shape[1] // (nx + 1)
    rows = nx * group
    groups = count // group
    two, n = lax.axis_size("dir"), lax.axis_size("shard")
    slab = nx // n
    parts = min(2, slab)
    some = slab // parts
    width = lanes // two
    vmem = pl.BlockSpec(memory_space=pltpu.VMEM)
    half = jnp.bfloat16
    dma = pltpu.SemaphoreType.DMA
    return pl.pallas_call(
        functools.partial(chain_kernel, group, nx),
        out_shape=jax.ShapeDtypeStruct((slab, table.shape[0], width), jnp.float32),
        in_specs=[vmem] * 12,
        out_specs=vmem,
        scratch_shapes=[
            pltpu.VMEM((rows, lanes), half),
            pltpu.VMEM((rows + group, rows), half),
            pltpu.VMEM((1, groups, nx, group, lanes), half),
            pltpu.VMEM((groups, slab, n, group, lanes), half),
            pltpu.VMEM((two, groups, nx, group, width), half),
            pltpu.VMEM((parts, groups, n, some, group, lanes), half),
            pltpu.VMEM((groups, nx, group, lanes), half),
            pltpu.VMEM((parts, two, groups, n, some, group, width), half),
            dma((groups, parts, n)), dma((groups, parts, n)), dma((groups, parts)),
            dma((groups, slab, n)), dma((groups, slab, n)), dma((groups, slab)),
            dma((groups, parts, two * n)), dma((groups, parts, two * n)), dma((groups, parts)),
        ],
        compiler_params=pltpu.CompilerParams(
            vmem_limit_bytes=VMEM_LIMIT, collective_id=0, has_side_effects=True
        ),
    )(q, operator, *tables, basis, damping, analysis, synthesis, decay, table)


def mix(block, analysis_ref, synthesis_ref, decay_ref):
    harmonic = jnp.dot(analysis_ref[...], block, preferred_element_type=jnp.float32)
    harmonic = (harmonic * decay_ref[...]).astype(jnp.bfloat16)
    return jnp.dot(synthesis_ref[...], harmonic, preferred_element_type=jnp.float32)


def moment_table(orient, quad_weights):
    head_x, head_y, head_z = (orient[0], orient[1], orient[2])
    unity = jnp.ones_like(head_x)
    zero = jnp.zeros_like(head_x)
    moment_rows = [
        unity,
        head_x * head_x - one_third,
        head_y * head_y - one_third,
        head_x * head_y,
        head_x * head_z,
        head_y * head_z,
        zero,
        zero,
    ]
    return jnp.stack(moment_rows) * quad_weights[None, :]


def on_device(propagators, field, orient, quad_weights, analysis, synthesis, decay):
    state = propagators[0]
    count, nx, lanes = state.shape
    nz = lanes // NY
    group = min(16, count)
    groups = count // group
    basis = jnp.asarray(real_basis(NY, nz).astype(jnp.bfloat16))
    damping = jnp.exp(-field)
    harmonics, total = analysis.shape
    pad = -harmonics % 128

    def regroup(values, axis):
        shape = values.shape[:axis] + (-1, groups, group) + values.shape[axis + 1 :]
        values = jnp.swapaxes(values.reshape(shape), axis, axis + 1)
        return values.reshape(values.shape[:axis] + (total,) + values.shape[axis + 3 :])

    analysis = regroup(jnp.pad(analysis, ((0, pad), (0, 0))), 1)
    synthesis = regroup(jnp.pad(synthesis, ((0, 0), (0, pad))), 0)
    decay = jnp.pad(decay, (0, pad))[:, None]
    table = regroup(moment_table(orient, quad_weights), 1)
    heading = lax.dynamic_slice_in_dim(orient, lax.axis_index("shard") * count, count, 1)
    scale = (1.0 - 2.0 * lax.axis_index("dir").astype(jnp.float32)) * transport_length
    operator, nyquist = line_operator(heading, scale, nx, group)
    cu, su, cv, sv = plane_tables(heading, scale, NY, nz)
    tables = (cu, su, cv * nyquist, sv * nyquist)
    result = chain(state, operator, tables, basis, damping, analysis, synthesis, decay, table)
    return result[:, 0], jnp.moveaxis(result[:, 1:6], 1, 0)


def solution(mesh):
    in_specs = (P("dir", "shard", None, None), P(), P(), P(), P(), P(), P())
    out_specs = (P("shard", "dir"), P(None, "shard", "dir"))
    return jax.shard_map(
        on_device, mesh=mesh, in_specs=in_specs, out_specs=out_specs, check_vma=False
    )
```

time: 377 us -> 316 us (0.84)
  Pallas kernels: 66.5 us -> 297 us
  waiting for transfers between devices: 181 us -> 0 us
  blocking collectives: 97 us -> 0 us
  starting transfers between devices: 12.1 us -> 0 us
    pallas_call x4 -> x1, Pallas kernels: 66.5 us -> 297 us  [chain(): pl.pallas_call(functools.partial(chain_kernel, group, nx), out_shape=jax....]
    all_to_all x2 -> x0, waiting for transfers between devices: 181 us -> none  [the longest x1 91.6 us: on_device(): moved = lax.all_to_all(moved, ('dir', 'shard'), 0, 0, tiled=True)]
    all_to_all x1 -> x0, blocking collectives: 97 us -> none  [on_device(): mixed = lax.all_to_all(mixed, 'shard', 0, 0, tiled=True)]
    all_to_all x2 -> x0, starting transfers between devices: 12.1 us -> none  [the longest x1 6.6 us: on_device(): moved = lax.all_to_all(moved, 'shard', 0, 0, tiled=True)]
  transfers between devices with their start and end apart: 2 -> 0, of which waited for: 2 -> 0; matrix products, arithmetic and copies ran while one was open for 1% -> 0% of each run, Pallas kernels for 0% -> 0%
where the time goes in v3:
time: 316 us; the launch traced here: 315 us
  Pallas kernels  297 us (94%)
  local copies, waits for them, and re-layouts  8.5 us (3%)
  other arithmetic  5.32 us (2%)
    pallas_call x1, Pallas kernels, chain(): pl.pallas_call(functools.partial(chain_kernel, group, nx), out_shape=jax....  297 us

profile of v3, /device:TPU:19, one launch (start us, length us, event | category | flops | bytes accessed | tf_op | source)
XLA Modules:
  0.0 314.8 jit_solution(8269585167353356468)
XLA Ops:
  0.6 0.0 copy-start.6
  0.6 0.8 constant_dynamic-slice_fusion
  1.4 0.1 multiply_bitcast_fusion.1
  1.5 2.8 fusion.23
  4.2 0.1 mul.240
  4.3 0.8 multiply_cosine_fusion.2
  5.1 0.1 cos.30
  5.2 0.0 copy-start
  5.3 2.8 convolution_convert_fusion
  8.1 0.9 pad_maximum_fusion.p_ref
  9.0 0.1 stack.21
  9.1 0.1 stack.22
  9.2 0.1 stack.23
  9.3 0.1 stack.24
  9.4 0.1 stack.25
  9.6 0.1 mul.281
  9.7 0.7 reshape.146.table_ref
  10.4 0.2 copy.30
  10.6 0.1 pad.12
  10.7 0.0 copy-start.5
  10.7 0.0 copy-start.2
  10.7 1.0 copy.40.analysis_ref
  11.8 0.2 copy.32
  12.0 0.1 pad.13
  12.0 0.8 copy.33
  12.9 0.9 copy.41.decay_ref
  13.8 0.7 negate_exponential_fusion.damping_ref
  14.5 297.4 %shard_map.185 = f32[4,8,512]{2,1,0:T(8,128)} custom-call(bf16[32,64,1024]{2,1,0:T(8,128)(2,1)} %bitcast.36, bf16[2,1040,64]{2,1,0:T(8,128)(2,1)} %pad_maximum_fusion.p_ref, f32[32,1024]{1,0:T(8,128)} %get-tuple-element.16.c_ref, f32[32,1024]{1,0:T(8,128)} %get-tuple-element.14.s_ref, f32[32,1024]{1,0:T(8,128)} %get-tuple-element.15.cv_ref, ...), custom_call_target="tpu_custom_call" | custom-call | tf_op jit(solution)/shard_map/pallas_call | solution.py:424
  311.9 0.8 slice_bitcast_fusion
  312.7 0.6 copy.42
  313.4 0.8 slice.31
  314.2 0.6 copy.51
  (24 shorter events, 0.2 us)
Async XLA Ops:
  0.6 7.4 %copy-start.6 = (bf16[64]{0:T(256)(128)(2,1)S(1)}, bf16[64]{0:T(256)(128)(2,1)}, u32[]{:S(2)}) copy-start(bf16[64]{0:T(256)(128)(2,1)} %constant.78) | copy-start | bytes 388
  1.5 7.5 %copy-start.3 = (f32[3,512]{1,0:T(4,128)S(1)}, f32[3,512]{1,0:T(4,128)}, u32[]{:S(2)}) copy-start(f32[3,512]{1,0:T(4,128)} %param.20) | copy-start | bytes 18436
  4.2 5.3 %copy-start.4 = (f32[512]{0:T(512)S(1)}, f32[512]{0:T(512)}, u32[]{:S(2)}) copy-start(f32[512]{0:T(512)} %param.21) | copy-start | bytes 6148
  5.2 5.2 %copy-start = (bf16[441,512]{1,0:T(8,128)(2,1)S(1)}, bf16[441,512]{1,0:T(8,128)(2,1)}, u32[]{:S(2)}) copy-start(bf16[441,512]{1,0:T(8,128)(2,1)} %param.22) | copy-start | bytes 1354756
  10.4 1.4 copy-start.1
  10.7 2.2 copy-start.5
  10.7 3.0 copy-start.2
